TPU v7x, 128 devices: a whole 4x4x4 slice. The times are simulated.
128 devices in a mesh: gx: 16 (over z, x_hi, core), gy: 8 (over y, x_lo).
Axes of the slice: x: 4 (x_hi: 2, x_lo: 2; x = x_hi * 2 + x_lo), y: 4, z: 4, core: 2. Of those that a mesh axis runs over, the one named last changes fastest.
Arguments:
- pressure: float32 [256, 128, 512], P('gx', 'gy'), may hold values from -6 to 6
- divergence: float32 [256, 128, 512], P('gx', 'gy'), may hold values from -8 to 8
- inverse_density: float32 [256, 128, 512], P('gx', 'gy'), may hold values from 0.2 to 5
Outputs:
- new_pressure: float32 [256, 128, 512], P('gx', 'gy')
All inputs are finite; a program needn't handle non-finite values.
Results may differ from a plain program's by a relative error of at most 0.000021.
Values sent between devices are 32-bit elements; how exact they have to be, the bound alone decides.
A program may use at most 320 MiB of HBM per device.

v0:
```python
import functools

import jax
import jax.numpy as jnp
from jax import lax
from jax.experimental import pallas as pl
from jax.experimental.pallas import tpu as pltpu
from jax.sharding import PartitionSpec as P

MESH = pl.DeviceIdType.MESH
F32 = jnp.float32
BF16 = jnp.bfloat16

S1 = 0.05
S2 = 0.2
S3 = 0.8
MIDPOINT = (2.0 + 0.3) / 2
HALFWIDTH = (2.0 - 0.3) / 2
SIGMA = MIDPOINT / HALFWIDTH
P1 = 1.0 / SIGMA
P2 = 1.0 / (2.0 * SIGMA - P1)
CA = P2 * P1
CB = 2.0 * P2 / HALFWIDTH
NEAR = [(-1, 0), (1, 0), (0, -1), (0, 1), (-1, -1), (-1, 1), (1, -1), (1, 1)]


def thirds(x):
    high = x.astype(BF16)
    rest = x - high.astype(F32)
    middle = rest.astype(BF16)
    low = (rest - middle.astype(F32)).astype(BF16)
    return high, middle, low


def exact_dot(x, matrix):
    total = None
    for part in thirds(x):
        term = jnp.dot(part, matrix, preferred_element_type=F32)
        total = term if total is None else total + term
    return total


def z_next(v):
    half = v.shape[1] // 2
    return jnp.concatenate([v[:, half:], pltpu.roll(v[:, :half], half - 1, 1)], axis=1)


def z_before(v):
    half = v.shape[1] // 2
    return jnp.concatenate([pltpu.roll(v[:, half:], 1, 1), v[:, :half]], axis=1)


def weighted_sum(f):
    q = pltpu.roll(f, 1, 2) + pltpu.roll(f, f.shape[2] - 1, 2)
    face = 0.5 * f + 0.125 * q
    edge = 0.125 * f + 0.0625 * q
    rows = f.shape[1]
    a = 0.5 * q + (pltpu.roll(face, 1, 1) + pltpu.roll(face, rows - 1, 1))
    b = face + (pltpu.roll(edge, 1, 1) + pltpu.roll(edge, rows - 1, 1))
    return a[1:-1] + (b[:-2] + b[2:])


def coarse_operator(v, mob, mob_sum):
    c = v[1:-1]
    m = mob[1:-1]
    return S3 * c + 0.5 * (
        5.0 * m * c - m * weighted_sum(v) + c * mob_sum - weighted_sum(mob * v)
    )


def kernel(
    nx, ny,
    p_hbm, d_hbm, m_hbm, o_hbm,
    px, mf, u, u2, d, r, out, kx, kyl, kyh, kz, w,
    ystage, yrecv, pair, rs, tmat, pmat, pin, pout,
    mid_b, mid_stage, mid_rx, mid_ry, mid_rc, b2, m2, w2, kx2, kyl2, kyh2, kz2,
    va, vb, rr, x2, xk,
    cstage, crecv, cm, cw, cb, ce, t2,
    fstage, frecv, fk,
    ar1, ar2,
    in_sem, out_sem, fs, fr, ms, mr, cs, cr, xs, xr, as1, ar1s, as2, ar2s,
):
    gx = lax.axis_index("gx")
    gy = lax.axis_index("gy")

    def device(ox, oy):
        return (lax.rem(gx + (ox % nx), nx), lax.rem(gy + (oy % ny), ny))

    peers = {(o, 0) for o in range(1, nx)} | {(0, o) for o in range(1, ny)}
    peers |= {(dx % nx, dy % ny) for dx, dy in NEAR}
    peers = sorted(peers - {(0, 0)})

    loads = [
        pltpu.make_async_copy(m_hbm, mf.at[1:17, 8:24, :], in_sem.at[0]),
        pltpu.make_async_copy(p_hbm, px.at[1:17, 8:24, :], in_sem.at[1]),
        pltpu.make_async_copy(d_hbm, d, in_sem.at[2]),
    ]
    for c in loads:
        c.start()
    barrier = pltpu.get_barrier_semaphore()
    for ox, oy in peers:
        pl.semaphore_signal(barrier, inc=1, device_id=device(ox, oy), device_id_type=MESH)

    zi = lax.broadcasted_iota(jnp.int32, tmat.shape, 0)
    ci = lax.broadcasted_iota(jnp.int32, tmat.shape, 1)
    hit = (zi >> 1) == (((ci & 127) << 1) + (ci >> 7))
    tmat[...] = jnp.where(hit, 1.0, 0.0).astype(BF16)
    zi = lax.broadcasted_iota(jnp.int32, pmat.shape, 1)
    ci = lax.broadcasted_iota(jnp.int32, pmat.shape, 0)
    hit = (zi >> 1) == (((ci & 127) << 1) + (ci >> 7))
    pmat[...] = jnp.where(hit, 1.0, 0.0).astype(BF16)
    pl.semaphore_wait(barrier, len(peers))

    def remote(src, dst, ssem, rsem, ox, oy):
        return pltpu.make_async_remote_copy(
            src_ref=src, dst_ref=dst, send_sem=ssem, recv_sem=rsem,
            device_id=device(ox, oy), device_id_type=MESH,
        )

    def fine_send(arr, n):
        for x in range(16):
            ystage[n, 0, x : x + 1, :] = arr[x + 1, 8:9, :]
            ystage[n, 1, x : x + 1, :] = arr[x + 1, 23:24, :]
        copies = [
            remote(arr.at[1, 8:24, :], arr.at[17, 8:24, :], fs.at[n, 0], fr.at[n, 0], -1, 0),
            remote(arr.at[16, 8:24, :], arr.at[0, 8:24, :], fs.at[n, 1], fr.at[n, 1], 1, 0),
            remote(ystage.at[n, 0], yrecv.at[n, 1], fs.at[n, 2], fr.at[n, 2], 0, -1),
            remote(ystage.at[n, 1], yrecv.at[n, 0], fs.at[n, 3], fr.at[n, 3], 0, 1),
        ]
        for c in copies:
            c.start()
        return copies

    def fine_rows(arr, n):
        for x in range(16):
            arr[x + 1, 7:8, :] = yrecv[n, 0, x : x + 1, :]
            arr[x + 1, 24:25, :] = yrecv[n, 1, x : x + 1, :]

    def fine_wait(copies, arr, n):
        for c in copies:
            c.wait()
        fine_rows(arr, n)

    def restrict_fine(get, scale):
        def body(j, carry):
            both = get(2 * j) + get(2 * j + 1)
            for t in range(4):
                lanes = slice(128 * t, 128 * t + 128)
                pair[t] = both[:, lanes]
                rs[j, :, lanes] = pair[t, pl.ds(0, 8, stride=2), :] + pair[t, pl.ds(1, 8, stride=2), :]
            return carry

        lax.fori_loop(0, 8, body, 0)
        got = exact_dot(rs[...].reshape(64, 512), tmat[...]) * scale
        return got.reshape(8, 8, 256)

    def mid_send(n):
        low = lax.broadcasted_iota(jnp.int32, (8, 256), 0) < 4
        for t in range(4):
            a = mid_b[n, 2 * t]
            b = mid_b[n, 2 * t + 1]
            mid_stage[n, 0, t] = jnp.where(low, a, pltpu.roll(b, 4, 0))
            mid_stage[n, 1, t] = jnp.where(low, pltpu.roll(a, 4, 0), b)
        copies = [
            remote(mid_b.at[n, 0:4], mid_rx.at[n, 1], ms.at[n, 0], mr.at[n, 0], -1, 0),
            remote(mid_b.at[n, 4:8], mid_rx.at[n, 0], ms.at[n, 1], mr.at[n, 1], 1, 0),
            remote(mid_stage.at[n, 0], mid_ry.at[n, 1], ms.at[n, 2], mr.at[n, 2], 0, -1),
            remote(mid_stage.at[n, 1], mid_ry.at[n, 0], ms.at[n, 3], mr.at[n, 3], 0, 1),
        ]
        k = 4
        for i, dx in enumerate((-1, 1)):
            for j, dy in enumerate((-1, 1)):
                copies.append(
                    remote(
                        mid_stage.at[n, j, 2 * i : 2 * i + 2], mid_rc.at[n, 1 - i, 1 - j],
                        ms.at[n, k], mr.at[n, k], dx, dy,
                    )
                )
                k += 1
        for c in copies:
            c.start()
        return copies

    def mid_wait(copies, n, ext):
        for x in range(8):
            ext[4 + x, 4:12, :] = mid_b[n, x]
        for c in copies:
            c.wait()
        for i in range(2):
            for x in range(4):
                ext[12 * i + x, 4:12, :] = mid_rx[n, i, x]
            for t in range(4):
                for q in range(2):
                    ext[4 + 2 * t + q, 12 * i : 12 * i + 4, :] = mid_ry[n, i, t, 4 * q : 4 * q + 4, :]
            for j in range(2):
                for t in range(2):
                    for q in range(2):
                        ext[12 * i + 2 * t + q, 12 * j : 12 * j + 4, :] = mid_rc[
                            n, i, j, t, 4 * q : 4 * q + 4, :
                        ]

    def coarse_block(get, n, scale):
        for x in range(4):
            a = get(4 + 2 * x) + get(5 + 2 * x)
            t2[x] = (a[:, :128] + a[:, 128:]) * scale
            cstage[n, 4 * x : 4 * x + 4, :] = (
                t2[x, pl.ds(4, 4, stride=2), :] + t2[x, pl.ds(5, 4, stride=2), :]
            )

    def coarse_send(n):
        copies = []
        for k, (dx, dy) in enumerate(NEAR):
            copies.append(
                remote(cstage.at[n], crecv.at[n, k], cs.at[n, k], cr.at[n, k], dx, dy)
            )
            copies[-1].start()
        return copies

    def coarse_wait(copies, n, ext):
        def place(dx, dy, block):
            for x in range(4):
                ext[4 * dx + 4 + x, 4 * dy + 4 : 4 * dy + 8, :] = block[4 * x : 4 * x + 4, :]

        place(0, 0, cstage.at[n])
        for c in copies:
            c.wait()
        for k, (dx, dy) in enumerate(NEAR):
            place(-dx, -dy, crecv.at[n, k])

    def fine_apply(arr, i, flux):
        c = arr[i + 1, 8:24, :]
        above = kx[i + 1] * (c - arr[i + 2, 8:24, :])
        fz = kz[i] * (c - pltpu.roll(c, 511, 1))
        total = S1 * c + (above - flux)
        total = total + kyl[i] * (c - arr[i + 1, 7:23, :])
        total = total + kyh[i] * (c - arr[i + 1, 9:25, :])
        total = total + (fz - pltpu.roll(fz, 1, 1))
        return c, total, above

    def first_flux(arr):
        return kx[0] * (arr[0, 8:24, :] - arr[1, 8:24, :])

    def mid_apply(arr, i):
        c = arr[i]
        total = S2 * c + kx2[i] * (c - arr[i - 1]) + kx2[i + 1] * (c - arr[i + 1])
        total = total + kyl2[i] * (c - pltpu.roll(c, 1, 0))
        total = total + kyh2[i] * (c - pltpu.roll(c, 15, 0))
        fz = kz2[i] * (c - z_next(c))
        return c, total + (fz - z_before(fz))

    def planes(start, stop, body):
        lax.fori_loop(start, stop, lambda i, carry: (body(i), carry)[1], 0)

    loads[0].wait()
    m_copies = fine_send(mf, 0)
    loads[1].wait()
    p_copies = fine_send(px, 1)
    mid_b[0] = restrict_fine(lambda i: mf[i + 1, 8:24, :], 0.125)
    m2_copies = mid_send(0)
    fine_wait(m_copies, mf, 0)

    def coefficients(i, carry):
        c = mf[i + 1, 8:24, :]
        below = 0.5 * (c + mf[i, 8:24, :])
        above = 0.5 * (c + mf[i + 2, 8:24, :])
        left = 0.5 * (c + mf[i + 1, 7:23, :])
        right = 0.5 * (c + mf[i + 1, 9:25, :])
        nxt = 0.5 * (c + pltpu.roll(c, 511, 1))
        kx[i] = below
        kx[i + 1] = above
        kyl[i] = left
        kyh[i] = right
        kz[i] = nxt
        w[i] = 1.0 / (S1 + below + above + left + right + nxt + pltpu.roll(nxt, 1, 1))
        return carry

    lax.fori_loop(0, 16, coefficients, 0)
    fine_wait(p_copies, px, 1)
    loads[2].wait()

    def pass_one(i, flux):
        c, total, above = fine_apply(px, i, flux)
        res = d[i] - total
        r[i] = res
        u[i + 1, 8:24, :] = w[i] * res * (1.0 / MIDPOINT)
        return above

    lax.fori_loop(0, 16, pass_one, first_flux(px))
    u_copies = fine_send(u, 2)

    mid_wait(m2_copies, 0, m2)
    coarse_block(lambda i: m2[i], 0, 0.125)
    m3_copies = coarse_send(0)

    def mid_coefficients(i):
        c = m2[i]
        below = 0.5 * (c + m2[i - 1])
        above = 0.5 * (c + m2[i + 1])
        left = 0.5 * (c + pltpu.roll(c, 1, 0))
        right = 0.5 * (c + pltpu.roll(c, 15, 0))
        nxt = 0.5 * (c + z_next(c))
        kx2[i] = below
        kx2[i + 1] = above
        kyl2[i] = left
        kyh2[i] = right
        kz2[i] = nxt
        w2[i] = 1.0 / (S2 + below + above + left + right + nxt + z_before(nxt))

    planes(1, 15, mid_coefficients)
    fine_wait(u_copies, u, 2)

    def pass_two(i, flux):
        c, total, above = fine_apply(u, i, flux)
        res = r[i] - total
        r[i] = res
        step = CA * c + CB * w[i] * res
        u2[i + 1, 8:24, :] = step
        px[i + 1, 8:24, :] = px[i + 1, 8:24, :] + c + step
        return above

    lax.fori_loop(0, 16, pass_two, first_flux(u))
    u2_copies = fine_send(u2, 3)

    coarse_wait(m3_copies, 0, cm)
    mob = cm[...]
    mob_sum = weighted_sum(mob)
    cw[1:11] = 0.8 / (S3 + 0.5 * (5.0 * mob[1:-1] + mob_sum))
    for x in range(4):
        cstage[1, 4 * x : 4 * x + 4, :] = cw[4 + x, 4:8, :]
    w3_copies = coarse_send(1)

    def response_one(i):
        vb[i] = (-S2 / MIDPOINT) * w2[i]

    planes(1, 15, response_one)

    def response_two(i):
        c, total = mid_apply(vb, i)
        step = CA * c + CB * w2[i] * (-S2 - total)
        xk[i] = 1.0 + c + step

    planes(2, 14, response_two)
    for x in range(8):
        fk[2, x : x + 1, :] = xk[4 + x, 3:4, :]
        fk[3, x : x + 1, :] = xk[4 + x, 12:13, :]
    fk[0] = xk[3, 4:12, :]
    fk[1] = xk[12, 4:12, :]
    fine_wait(u2_copies, u2, 3)

    def residual_plane(i, flux):
        c, total, above = fine_apply(u2, i, flux)
        r[i] = r[i] - total
        return above

    lax.fori_loop(0, 16, residual_plane, first_flux(u2))
    mid_b[1] = restrict_fine(lambda i: r[i], 0.5)
    b2_copies = mid_send(1)

    coarse_wait(w3_copies, 1, cw)
    weight = cw[...]
    y = jnp.ones_like(weight)
    psi = y
    lap = weighted_sum(mob)
    for k in range(3):
        cut = k + 1
        inner = slice(k, 12 - k)
        y = y[1:-1] - coarse_operator(
            weight[inner] * y, mob[inner], lap[k : 10 - k]
        )
        psi = psi[1:-1] + y
    functional = 1.0 - S3 * (weight[4:8] * psi[1:5])
    ce[0:4] = functional
    for plane in (0, 17):
        px[plane, 8:24, :] = px[plane, 8:24, :] + u[plane, 8:24, :] + u2[plane, 8:24, :]
    yrecv[1] = yrecv[1] + yrecv[2] + yrecv[3]
    mid_wait(b2_copies, 1, b2)

    def mid_one(i):
        va[i] = w2[i] * b2[i] * (1.0 / MIDPOINT)

    planes(1, 15, mid_one)

    def mid_two(i):
        c, total = mid_apply(va, i)
        res = b2[i] - total
        step = CA * c + CB * w2[i] * res
        rr[i] = res
        vb[i] = step
        x2[i] = c + step

    planes(2, 14, mid_two)

    def mid_three(i):
        c, total = mid_apply(vb, i)
        rr[i] = rr[i] - total

    planes(4, 12, mid_three)
    coarse_block(lambda i: rr[i], 2, 0.5)
    b3_copies = coarse_send(2)

    part = jnp.zeros((1, 128), F32)
    partm = jnp.zeros((1, 128), F32)
    for x in range(4):
        part = part + jnp.sum(
            ce[x, 4:8, :] * cstage[2, 4 * x : 4 * x + 4, :], axis=0, keepdims=True
        )
        partm = partm + jnp.sum(cstage[0, 4 * x : 4 * x + 4, :], axis=0, keepdims=True)
    row = lax.broadcasted_iota(jnp.int32, (8, 128), 0)
    ar1[0] = jnp.where(row < 1, part, partm)
    sums = []
    for o in range(1, nx):
        sums.append(remote(ar1.at[0], ar1.at[o], as1.at[o], ar1s.at[o], o, 0))
        sums[-1].start()

    coarse_wait(b3_copies, 2, cb)
    rhs = cb[...]
    e = weight * rhs
    for k in range(3):
        inner = slice(k, 12 - k)
        e = e[1:-1] + weight[k + 1 : 11 - k] * (
            rhs[k + 1 : 11 - k] - coarse_operator(e, mob[inner], lap[k : 10 - k])
        )
    for c in sums:
        c.wait()
    total = ar1[0]
    for o in range(1, nx):
        total = total + ar1[o]
    ar2[0] = total
    sums = []
    for o in range(1, ny):
        sums.append(remote(ar2.at[0], ar2.at[o], as2.at[o], ar2s.at[o], 0, o))
        sums[-1].start()

    ce[3:9] = e
    for x in range(6):
        for t in range(2):
            t2[x, pl.ds(t, 8, stride=2), :] = ce[3 + x, 2:10, :]
    for x in range(6):
        v = t2[x]
        both = jnp.concatenate([v, v], axis=1)
        for q in range(2):
            va[2 + 2 * x + q] = x2[2 + 2 * x + q] + both

    def post_one(i):
        c, tot = mid_apply(va, i)
        res = b2[i] - tot
        rr[i] = res
        vb[i] = w2[i] * res * (1.0 / MIDPOINT)

    planes(3, 13, post_one)

    def post_two(i):
        c, tot = mid_apply(vb, i)
        res = rr[i] - tot
        va[i] = va[i] + c + CA * c + CB * w2[i] * res

    planes(4, 12, post_two)
    for x in range(8):
        pin[8 * x : 8 * x + 8, :] = va[4 + x, 4:12, :]
        fstage[0, x : x + 1, :] = va[4 + x, 4:5, :]
        fstage[1, x : x + 1, :] = va[4 + x, 11:12, :]
    x_copies = [
        remote(pin.at[0:8], frecv.at[1], xs.at[0], xr.at[0], -1, 0),
        remote(pin.at[56:64], frecv.at[0], xs.at[1], xr.at[1], 1, 0),
        remote(fstage.at[0], frecv.at[3], xs.at[2], xr.at[2], 0, -1),
        remote(fstage.at[1], frecv.at[2], xs.at[3], xr.at[3], 0, 1),
    ]
    for c in x_copies:
        c.start()
    for c in sums:
        c.wait()
    total = ar2[0]
    for o in range(1, ny):
        total = total + ar2[o]
    cells = 16.0 * 128.0 * nx * ny
    sum_f = jnp.sum(total[0:1, :], axis=1, keepdims=True)
    sum_m = jnp.sum(total[1:2, :], axis=1, keepdims=True)
    kappa = 0.8 * (sum_f / cells) / (S3 + 5.0 * (sum_m / cells))
    for c in x_copies:
        c.wait()
    for x in range(8):
        pin2 = pin[8 * x : 8 * x + 8, :] + kappa * xk[4 + x, 4:12, :]
        pout[8 * x : 8 * x + 8, 0:256] = pin2
    for f in range(4):
        pout[64 + 8 * f : 72 + 8 * f, 0:256] = frecv[f] + kappa * fk[f]
    grown = exact_dot(pout[:, 0:256], pmat[...])
    pout[...] = grown

    def doubled(rows, t):
        v = pout[rows, 128 * t : 128 * t + 128]
        pair[t, pl.ds(0, 8, stride=2), :] = v
        pair[t, pl.ds(1, 8, stride=2), :] = v
        return pair[t]

    def add_planes(j, carry):
        for t in range(4):
            lanes = slice(128 * t, 128 * t + 128)
            v = doubled(pl.ds(pl.multiple_of(8 * j, 8), 8), t)
            for q in range(2):
                px[2 * j + 1 + q, 8:24, lanes] = px[2 * j + 1 + q, 8:24, lanes] + v
        return carry

    lax.fori_loop(0, 8, add_planes, 0)
    for t in range(4):
        lanes = slice(128 * t, 128 * t + 128)
        for f in range(2):
            v = doubled(slice(64 + 8 * f, 72 + 8 * f), t)
            px[17 * f, 8:24, lanes] = px[17 * f, 8:24, lanes] + v
        for f in range(2):
            v = doubled(slice(80 + 8 * f, 88 + 8 * f), t)
            yrecv[1, f, :, lanes] = yrecv[1, f, :, lanes] + v
    fine_rows(px, 1)

    lax.fori_loop(0, 16, pass_one, first_flux(px))
    copies = fine_send(u, 4)
    fine_wait(copies, u, 4)

    def pass_last(i, flux):
        c, tot, above = fine_apply(u, i, flux)
        res = r[i] - tot
        out[i] = px[i + 1, 8:24, :] + c + CA * c + CB * w[i] * res
        return above

    lax.fori_loop(0, 16, pass_last, first_flux(u))
    store = pltpu.make_async_copy(out, o_hbm, out_sem.at[0])
    store.start()
    store.wait()


def solution(mesh):
    nx, ny = mesh.shape["gx"], mesh.shape["gy"]

    def local(p, d, m):
        vm = lambda *s: pltpu.VMEM(s, F32)
        sem = lambda *s: pltpu.SemaphoreType.DMA(s)
        scratch = [
            vm(18, 32, 512), vm(18, 32, 512), vm(18, 32, 512), vm(18, 32, 512),
            vm(16, 16, 512), vm(16, 16, 512), vm(16, 16, 512),
            vm(17, 16, 512), vm(16, 16, 512), vm(16, 16, 512), vm(16, 16, 512), vm(16, 16, 512),
            vm(5, 2, 16, 512), vm(5, 2, 16, 512), vm(4, 16, 128), vm(8, 8, 512),
            pltpu.VMEM((512, 256), BF16), pltpu.VMEM((256, 512), BF16), vm(64, 256), vm(96, 512),
            vm(2, 8, 8, 256), vm(2, 2, 4, 8, 256), vm(2, 2, 4, 8, 256), vm(2, 2, 4, 8, 256),
            vm(2, 2, 2, 2, 8, 256),
            vm(16, 16, 256), vm(16, 16, 256), vm(16, 16, 256), vm(17, 16, 256),
            vm(16, 16, 256), vm(16, 16, 256), vm(16, 16, 256),
            vm(16, 16, 256), vm(16, 16, 256), vm(16, 16, 256), vm(16, 16, 256), vm(16, 16, 256),
            vm(3, 16, 128), vm(3, 8, 16, 128), vm(12, 16, 128), vm(12, 16, 128), vm(12, 16, 128),
            vm(12, 16, 128), vm(6, 16, 128),
            vm(2, 8, 256), vm(4, 8, 256), vm(4, 8, 256),
            vm(nx, 8, 128), vm(ny, 8, 128),
            sem(3), sem(1), sem(5, 4), sem(5, 4), sem(2, 8), sem(2, 8), sem(3, 8), sem(3, 8),
            sem(4), sem(4), sem(nx), sem(nx), sem(ny), sem(ny),
        ]
        return pl.pallas_call(
            functools.partial(kernel, nx, ny),
            out_shape=jax.ShapeDtypeStruct((16, 16, 512), F32),
            in_specs=[pl.BlockSpec(memory_space=pl.ANY)] * 3,
            out_specs=pl.BlockSpec(memory_space=pl.ANY),
            scratch_shapes=scratch,
            compiler_params=pltpu.CompilerParams(collective_id=0, has_side_effects=True),
        )(p, d, m)

    spec = P("gx", "gy", None)
    return jax.shard_map(
        local, mesh=mesh, in_specs=(spec, spec, spec), out_specs=spec, check_vma=False
    )
```

profile of v0, /device:TPU:1, one launch (start us, length us, event | category | flops | bytes accessed | tf_op | source)
XLA Modules:
  0.0 67.9 jit_solution(6430635422205088939)
XLA Ops:
  0.0 66.0 %shard_map.37 = f32[16,16,512]{2,1,0:T(8,128)} custom-call(f32[16,16,512]{2,1,0:T(8,128)} %p_hbm.1, f32[16,16,512]{2,1,0:T(8,128)} %d_hbm.1, f32[16,16,512]{2,1,0:T(8,128)} %m_hbm.1), custom_call_target="tpu_custom_call" | custom-call | tf_op jit(solution)/shard_map/pallas_call | solution.py:554
  66.0 1.9 %copy.5 = f32[16,16,512]{2,1,0:T(8,128)} copy(f32[16,16,512]{2,1,0:T(8,128)} %shard_map.37) | data formatting | bytes 1048576
where the time goes:
time: 69 us; the launch traced here: 67.9 us
  Pallas kernels  66 us (96%)
  local copies, waits for them, and re-layouts  1.88 us (3%)
    pallas_call x1, Pallas kernels, local(): pl.pallas_call(functools.partial(kernel, nx, ny), out_shape=jax.ShapeDtyp...  66 us
    unnamed x1, local copies, waits for them, and re-layouts  1.88 us

commit v1 on v0

v1 whole, which is shorter than its diff:
```python
import functools

import jax
import jax.numpy as jnp
from jax import lax
from jax.experimental import pallas as pl
from jax.experimental.pallas import tpu as pltpu
from jax.sharding import PartitionSpec as P

MESH = pl.DeviceIdType.MESH
F32 = jnp.float32
BF16 = jnp.bfloat16

S1 = 0.05
S2 = 0.2
S3 = 0.8
MIDPOINT = (2.0 + 0.3) / 2
HALFWIDTH = (2.0 - 0.3) / 2
SIGMA = MIDPOINT / HALFWIDTH
P1 = 1.0 / SIGMA
P2 = 1.0 / (2.0 * SIGMA - P1)
CA = P2 * P1
CB = 2.0 * P2 / HALFWIDTH
INV = 1.0 / MIDPOINT
ALPHA = CA + CB * (MIDPOINT - 1.0)
STEP = CB * MIDPOINT
BETA = 1.0 / CB - 1.0
GAMMA = CA / CB
NEAR = [(-1, 0), (1, 0), (0, -1), (0, 1), (-1, -1), (-1, 1), (1, -1), (1, 1)]


def thirds(x):
    high = x.astype(BF16)
    rest = x - high.astype(F32)
    middle = rest.astype(BF16)
    low = (rest - middle.astype(F32)).astype(BF16)
    return high, middle, low


def exact_dot(x, matrix):
    total = None
    for part in thirds(x):
        term = jnp.dot(part, matrix, preferred_element_type=F32)
        total = term if total is None else total + term
    return total


def weighted_sum(f):
    q = pltpu.roll(f, 1, 2) + pltpu.roll(f, f.shape[2] - 1, 2)
    face = 0.5 * f + 0.125 * q
    edge = 0.125 * f + 0.0625 * q
    rows = f.shape[1]
    a = 0.5 * q + (pltpu.roll(face, 1, 1) + pltpu.roll(face, rows - 1, 1))
    b = face + (pltpu.roll(edge, 1, 1) + pltpu.roll(edge, rows - 1, 1))
    return a[1:-1] + (b[:-2] + b[2:])


def coarse_operator(v, mob, mob_sum):
    c = v[1:-1]
    m = mob[1:-1]
    return S3 * c + 0.5 * (
        5.0 * m * c - m * weighted_sum(v) + c * mob_sum - weighted_sum(mob * v)
    )


def fine_next(v):
    turned = pltpu.roll(v, 127, 2)
    lane = lax.broadcasted_iota(jnp.int32, v.shape, 2)
    return jnp.where(lane == 127, jnp.concatenate([turned[1:], turned[:1]], axis=0), turned)


def fine_before(v):
    turned = pltpu.roll(v, 1, 2)
    lane = lax.broadcasted_iota(jnp.int32, v.shape, 2)
    return jnp.where(lane == 0, jnp.concatenate([turned[3:], turned[:3]], axis=0), turned)


def mid_next(v):
    return jnp.concatenate([v[1:], pltpu.roll(v[:1], 127, 2)], axis=0)


def mid_before(v):
    return jnp.concatenate([pltpu.roll(v[1:], 1, 2), v[:1]], axis=0)


def kernel(
    nx, ny,
    p_hbm, d_hbm, m_hbm, out,
    px, mf, u, u2, d, g, dg, w, kx, ky, kz,
    xr, ys, yr, kyf, gyf, gxf, dl, rs, tmat, pmat, pout,
    mid_b, mid_stage, mid_rx, mid_ry, mid_rc, b2, m2, w2, d2, kx2, ky2, kz2,
    va, vb, rr, x2, xk,
    cstage, crecv, cm, cw, cb, ce, t2,
    base, fstage, frecv, fk,
    ar1, ar2,
    in_sem, fs, fr, ms, mr, cs, cr, xs, xrs, as1, ar1s, as2, ar2s,
):
    gx = lax.axis_index("gx")
    gy = lax.axis_index("gy")
    IN = slice(8, 24)
    LO = slice(7, 23)
    HI = slice(9, 25)

    def device(ox, oy):
        return (lax.rem(gx + (ox % nx), nx), lax.rem(gy + (oy % ny), ny))

    peers = {(o, 0) for o in range(1, nx)} | {(0, o) for o in range(1, ny)}
    peers |= {(dx % nx, dy % ny) for dx, dy in NEAR}
    peers = sorted(peers - {(0, 0)})

    loads = []
    for n, (src, dst) in enumerate(
        ((m_hbm, mf.at[1:17, :, IN, :]), (p_hbm, px.at[1:17, :, IN, :]), (d_hbm, d))
    ):
        loads.append(
            [
                pltpu.make_async_copy(
                    src.at[:, :, 128 * t : 128 * t + 128], dst.at[:, t], in_sem.at[n, t]
                )
                for t in range(4)
            ]
        )
        for c in loads[-1]:
            c.start()
    barrier = pltpu.get_barrier_semaphore()
    for ox, oy in peers:
        pl.semaphore_signal(barrier, inc=1, device_id=device(ox, oy), device_id_type=MESH)

    def remote(src, dst, ssem, rsem, ox, oy):
        return pltpu.make_async_remote_copy(
            src_ref=src, dst_ref=dst, send_sem=ssem, recv_sem=rsem,
            device_id=device(ox, oy), device_id_type=MESH,
        )

    def planes(start, stop, width, body):
        def several(j, carry):
            for q in range(width):
                body(start + width * j + q)
            return carry

        lax.fori_loop(0, (stop - start) // width, several, 0)

    zeros = jnp.zeros((4, 8, 128), F32)
    rims = (mf, px, u, u2)
    for a in rims:
        for plane in (0, 17):
            a[plane, :, 8:16, :] = zeros
            a[plane, :, 16:24, :] = zeros

    def clear(i):
        for a in rims:
            a[i + 1, :, 0:8, :] = zeros
            a[i + 1, :, 24:32, :] = zeros
        ky[i, :, 0:8, :] = zeros

    planes(0, 16, 2, clear)

    zi = lax.broadcasted_iota(jnp.int32, tmat.shape, 0)
    ci = lax.broadcasted_iota(jnp.int32, tmat.shape, 1)
    hit = (zi >> 1) == (((ci & 127) << 1) + (ci >> 7))
    tmat[...] = jnp.where(hit, 1.0, 0.0).astype(BF16)
    zi = lax.broadcasted_iota(jnp.int32, pmat.shape, 1)
    ci = lax.broadcasted_iota(jnp.int32, pmat.shape, 0)
    hit = (zi >> 1) == (((ci & 127) << 1) + (ci >> 7))
    pmat[...] = jnp.where(hit, 1.0, 0.0).astype(BF16)

    def pack_rows(arr, n):
        for x in range(16):
            ys[n, 0, :, x : x + 1, :] = arr[x + 1, :, 8:9, :]
            ys[n, 1, :, x : x + 1, :] = arr[x + 1, :, 23:24, :]

    def fine_send(arr, n):
        copies = [
            remote(arr.at[1, :, IN, :], xr.at[n, 1], fs.at[n, 0], fr.at[n, 0], -1, 0),
            remote(arr.at[16, :, IN, :], xr.at[n, 0], fs.at[n, 1], fr.at[n, 1], 1, 0),
            remote(ys.at[n, 0], yr.at[n, 1], fs.at[n, 2], fr.at[n, 2], 0, -1),
            remote(ys.at[n, 1], yr.at[n, 0], fs.at[n, 3], fr.at[n, 3], 0, 1),
        ]
        for c in copies:
            c.start()
        return copies

    def wait(copies):
        for c in copies:
            c.wait()

    def restrict_fine(arr, off, row, scale):
        for j in range(8):
            for t in range(4):
                total = None
                for q in range(2):
                    for h in range(2):
                        part = arr[2 * j + q + off, t, pl.ds(row + h, 8, stride=2), :]
                        total = part if total is None else total + part
                rs[8 * j : 8 * j + 8, 128 * t : 128 * t + 128] = total * scale
        return exact_dot(rs[...], tmat[...])

    def mid_put(n, got):
        low = lax.broadcasted_iota(jnp.int32, (2, 8, 128), 1) < 4
        blocks = []
        for x in range(8):
            rows = got[8 * x : 8 * x + 8]
            v = jnp.stack([rows[:, :128], rows[:, 128:]], axis=0)
            mid_b[n, x] = v
            blocks.append(v)
        for t in range(4):
            a, b = blocks[2 * t], blocks[2 * t + 1]
            mid_stage[n, 0, t] = jnp.where(low, a, pltpu.roll(b, 4, 1))
            mid_stage[n, 1, t] = jnp.where(low, pltpu.roll(a, 4, 1), b)

    def mid_send(n):
        copies = [
            remote(mid_b.at[n, 0:4], mid_rx.at[n, 1], ms.at[n, 0], mr.at[n, 0], -1, 0),
            remote(mid_b.at[n, 4:8], mid_rx.at[n, 0], ms.at[n, 1], mr.at[n, 1], 1, 0),
            remote(mid_stage.at[n, 0], mid_ry.at[n, 1], ms.at[n, 2], mr.at[n, 2], 0, -1),
            remote(mid_stage.at[n, 1], mid_ry.at[n, 0], ms.at[n, 3], mr.at[n, 3], 0, 1),
        ]
        k = 4
        for i, dx in enumerate((-1, 1)):
            for j, dy in enumerate((-1, 1)):
                copies.append(
                    remote(
                        mid_stage.at[n, j, 2 * i : 2 * i + 2], mid_rc.at[n, 1 - i, 1 - j],
                        ms.at[n, k], mr.at[n, k], dx, dy,
                    )
                )
                k += 1
        for c in copies:
            c.start()
        return copies

    def mid_place(n, ext):
        for i in range(2):
            for x in range(4):
                ext[12 * i + x, :, 12:20, :] = mid_rx[n, i, x]
            for t in range(4):
                for q in range(2):
                    ext[4 + 2 * t + q, :, 8 + 12 * i : 12 + 12 * i, :] = mid_ry[
                        n, i, t, :, 4 * q : 4 * q + 4, :
                    ]
            for j in range(2):
                for t in range(2):
                    for q in range(2):
                        ext[12 * i + 2 * t + q, :, 8 + 12 * j : 12 + 12 * j, :] = mid_rc[
                            n, i, j, t, :, 4 * q : 4 * q + 4, :
                        ]

    def mid_own(n, ext):
        for x in range(8):
            ext[4 + x, :, 12:20, :] = mid_b[n, x]

    def coarse_block(arr, n, row, scale):
        for x in range(4):
            total = None
            for q in range(2):
                for t in range(2):
                    for h in range(2):
                        part = arr[4 + 2 * x + q, t, pl.ds(row + h, 4, stride=2), :]
                        total = part if total is None else total + part
            cstage[n, 4 * x : 4 * x + 4, :] = total * scale

    def coarse_send(n):
        copies = []
        for k, (dx, dy) in enumerate(NEAR):
            copies.append(
                remote(cstage.at[n], crecv.at[n, k], cs.at[n, k], cr.at[n, k], dx, dy)
            )
            copies[-1].start()
        return copies

    def coarse_wait(copies, n, ext):
        def place(dx, dy, block):
            for x in range(4):
                ext[4 * dx + 4 + x, 4 * dy + 4 : 4 * dy + 8, :] = block[4 * x : 4 * x + 4, :]

        place(0, 0, cstage.at[n])
        wait(copies)
        for k, (dx, dy) in enumerate(NEAR):
            place(-dx, -dy, crecv.at[n, k])

    def fine_sum(arr, i):
        c = arr[i + 1, :, IN, :]
        z = kz[i]
        total = kx[i] * arr[i, :, IN, :] + kx[i + 1] * arr[i + 2, :, IN, :]
        total = total + ky[i, :, LO, :] * arr[i + 1, :, LO, :]
        total = total + ky[i, :, IN, :] * arr[i + 1, :, HI, :]
        return c, total + z * fine_next(c) + fine_before(z * c)

    def mid_sum(arr, i):
        c = arr[i, :, IN, :]
        z = kz2[i]
        total = kx2[i] * arr[i - 1, :, IN, :] + kx2[i + 1] * arr[i + 1, :, IN, :]
        total = total + ky2[i, :, LO, :] * arr[i, :, LO, :]
        total = total + ky2[i, :, IN, :] * arr[i, :, HI, :]
        return c, total + z * mid_next(c) + mid_before(z * c)

    def add_rows(arr, off, row):
        for x in range(16):
            for f in range(2):
                k = row + 15 * f
                arr[x + off, :, k : k + 1, :] = (
                    arr[x + off, :, k : k + 1, :] + dl[f, :, x : x + 1, :]
                )

    wait(loads[0])
    pack_rows(mf, 0)
    mid_put(0, restrict_fine(mf, 1, 8, 0.125))
    wait(loads[1])
    pack_rows(px, 1)
    wait(loads[2])
    pl.semaphore_wait(barrier, len(peers))
    m_copies = fine_send(mf, 0)
    p_copies = fine_send(px, 1)
    m2_copies = mid_send(0)

    def coefficients(i):
        c = mf[i + 1, :, IN, :]
        below = 0.5 * (c + mf[i, :, IN, :])
        above = c + mf[i + 2, :, IN, :]
        left = c + mf[i + 1, :, LO, :]
        right = 0.5 * (c + mf[i + 1, :, HI, :])
        after = 0.5 * (c + fine_next(c))
        before = c + fine_before(c)
        kx[i] = below
        ky[i, :, IN, :] = right
        kz[i] = after
        dg[i] = (S1 + below + right + after) + 0.5 * (above + left + before)

    planes(0, 16, 4, coefficients)
    kx[16] = 0.5 * mf[16, :, IN, :]

    def first_sum(i):
        c, total = fine_sum(px, i)
        g[i] = d[i] + total

    planes(0, 16, 4, first_sum)

    wait(m_copies)
    for f in range(2):
        face = 0.5 * xr[0, f]
        kx[16 * f] = kx[16 * f] + face
        dg[15 * f] = dg[15 * f] + face
        face = 0.5 * yr[0, f]
        kyf[f] = 0.5 * ys[0, f] + face
        dl[f] = face
    add_rows(dg, 0, 0)
    wait(p_copies)
    for f in range(2):
        g[15 * f] = g[15 * f] + kx[16 * f] * xr[1, f]
        dl[f] = kyf[f] * yr[1, f]
    add_rows(g, 0, 0)

    def first_step(i):
        weight = INV / dg[i]
        w[i] = weight
        u[i + 1, :, IN, :] = weight * g[i] - INV * px[i + 1, :, IN, :]

    planes(0, 16, 4, first_step)
    pack_rows(u, 2)
    u_copies = fine_send(u, 2)

    def second_sum(i):
        c, total = fine_sum(u, i)
        u2[i + 1, :, IN, :] = ALPHA * c + STEP * (w[i] * total)

    planes(0, 16, 4, second_sum)
    for x in range(16):
        for f in range(2):
            gyf[f, :, x : x + 1, :] = w[x, :, 15 * f : 15 * f + 1, :]
    for f in range(2):
        gyf[f] = STEP * (gyf[f] * kyf[f])
        gxf[f] = STEP * (w[15 * f] * kx[16 * f])
    mid_own(0, m2)
    wait(m2_copies)
    mid_place(0, m2)
    coarse_block(m2, 0, 12, 0.125)
    m3_copies = coarse_send(0)

    wait(u_copies)
    for f in range(2):
        k = 1 + 15 * f
        u2[k, :, IN, :] = u2[k, :, IN, :] + gxf[f] * xr[2, f]
        dl[f] = gyf[f] * yr[2, f]
    add_rows(u2, 1, 8)
    pack_rows(u2, 3)
    u2_copies = fine_send(u2, 3)

    def third_sum(i):
        c, total = fine_sum(u2, i)
        before = u[i + 1, :, IN, :]
        g[i] = dg[i] * (BETA * c - GAMMA * before) + total
        px[i + 1, :, IN, :] = px[i + 1, :, IN, :] + before + c

    planes(0, 16, 4, third_sum)

    def mid_coefficients(i):
        c = m2[i, :, IN, :]
        below = 0.5 * (c + m2[i - 1, :, IN, :])
        above = 0.5 * (c + m2[i + 1, :, IN, :])
        left = c + m2[i, :, LO, :]
        right = 0.5 * (c + m2[i, :, HI, :])
        after = 0.5 * (c + mid_next(c))
        before = c + mid_before(c)
        kx2[i] = below
        kx2[i + 1] = above
        ky2[i, :, IN, :] = right
        kz2[i] = after
        diagonal = (S2 + below + above + right + after) + 0.5 * (left + before)
        d2[i] = diagonal
        w2[i] = INV / diagonal

    planes(1, 15, 7, mid_coefficients)
    coarse_wait(m3_copies, 0, cm)
    mob = cm[...]
    lap = weighted_sum(mob)
    cw[1:11] = 0.8 / (S3 + 0.5 * (5.0 * mob[1:-1] + lap))
    for x in range(4):
        cstage[1, 4 * x : 4 * x + 4, :] = cw[4 + x, 4:8, :]
    w3_copies = coarse_send(1)

    wait(u2_copies)
    for f in range(2):
        g[15 * f] = g[15 * f] + kx[16 * f] * xr[3, f]
        dl[f] = kyf[f] * yr[3, f]
    add_rows(g, 0, 0)
    mid_put(1, restrict_fine(g, 0, 0, 0.5))
    b2_copies = mid_send(1)

    def response_one(i):
        vb[i, :, IN, :] = (-S2) * w2[i]

    planes(1, 15, 7, response_one)

    def response_two(i):
        c, total = mid_sum(vb, i)
        xk[i] = 1.0 + (1.0 + ALPHA) * c + STEP * (w2[i] * total)

    planes(2, 14, 6, response_two)
    for x in range(8):
        fk[2, :, x : x + 1, :] = xk[4 + x, :, 3:4, :]
        fk[3, :, x : x + 1, :] = xk[4 + x, :, 12:13, :]
    fk[0] = xk[3, :, 4:12, :]
    fk[1] = xk[12, :, 4:12, :]
    coarse_wait(w3_copies, 1, cw)
    weight = cw[...]
    y = jnp.ones_like(weight)
    psi = y
    for k in range(3):
        inner = slice(k, 12 - k)
        y = y[1:-1] - coarse_operator(weight[inner] * y, mob[inner], lap[k : 10 - k])
        psi = psi[1:-1] + y
    ce[0:4] = 1.0 - S3 * (weight[4:8] * psi[1:5])
    for f in range(2):
        xr[1, f] = xr[1, f] + xr[2, f] + xr[3, f]
        yr[1, f] = yr[1, f] + yr[2, f] + yr[3, f]
    mid_own(1, b2)
    wait(b2_copies)
    mid_place(1, b2)

    def mid_one(i):
        va[i, :, IN, :] = w2[i] * b2[i, :, IN, :]

    planes(1, 15, 7, mid_one)

    def mid_two(i):
        c, total = mid_sum(va, i)
        step = ALPHA * c + STEP * (w2[i] * total)
        vb[i, :, IN, :] = step
        x2[i] = c + step

    planes(2, 14, 6, mid_two)

    def mid_three(i):
        c, total = mid_sum(vb, i)
        rr[i] = d2[i] * (BETA * c - GAMMA * va[i, :, IN, :]) + total

    planes(4, 12, 4, mid_three)
    coarse_block(rr, 2, 4, 0.5)
    b3_copies = coarse_send(2)

    part = jnp.zeros((1, 128), F32)
    partm = jnp.zeros((1, 128), F32)
    for x in range(4):
        part = part + jnp.sum(
            ce[x, 4:8, :] * cstage[2, 4 * x : 4 * x + 4, :], axis=0, keepdims=True
        )
        partm = partm + jnp.sum(cstage[0, 4 * x : 4 * x + 4, :], axis=0, keepdims=True)
    row = lax.broadcasted_iota(jnp.int32, (8, 128), 0)
    ar1[0] = jnp.where(row < 1, part, partm)
    sums = []
    for o in range(1, nx):
        sums.append(remote(ar1.at[0], ar1.at[o], as1.at[o], ar1s.at[o], o, 0))
        sums[-1].start()

    coarse_wait(b3_copies, 2, cb)
    rhs = cb[...]
    e = weight * rhs
    for k in range(3):
        inner = slice(k, 12 - k)
        e = e[1:-1] + weight[k + 1 : 11 - k] * (
            rhs[k + 1 : 11 - k] - coarse_operator(e, mob[inner], lap[k : 10 - k])
        )
    wait(sums)
    total = ar1[0]
    for o in range(1, nx):
        total = total + ar1[o]
    ar2[0] = total
    sums = []
    for o in range(1, ny):
        sums.append(remote(ar2.at[0], ar2.at[o], as2.at[o], ar2s.at[o], 0, o))
        sums[-1].start()

    ce[3:9] = e
    for x in range(6):
        for h in range(2):
            t2[x, pl.ds(h, 8, stride=2), :] = ce[3 + x, 2:10, :]
    for x in range(6):
        v = t2[x]
        both = jnp.stack([v, v], axis=0)
        for q in range(2):
            va[2 + 2 * x + q, :, IN, :] = x2[2 + 2 * x + q] + both

    def post_one(i):
        c, total = mid_sum(va, i)
        vb[i, :, IN, :] = w2[i] * (b2[i, :, IN, :] + total) - INV * c

    planes(3, 13, 5, post_one)

    def post_two(i):
        c, total = mid_sum(vb, i)
        done = va[i, :, IN, :] + (1.0 + ALPHA) * c + STEP * (w2[i] * total)
        base[i - 4] = done[:, 4:12, :]

    planes(4, 12, 4, post_two)
    for x in range(8):
        fstage[0, :, x : x + 1, :] = base[x, :, 0:1, :]
        fstage[1, :, x : x + 1, :] = base[x, :, 7:8, :]
    x_copies = [
        remote(base.at[0], frecv.at[1], xs.at[0], xrs.at[0], -1, 0),
        remote(base.at[7], frecv.at[0], xs.at[1], xrs.at[1], 1, 0),
        remote(fstage.at[0], frecv.at[3], xs.at[2], xrs.at[2], 0, -1),
        remote(fstage.at[1], frecv.at[2], xs.at[3], xrs.at[3], 0, 1),
    ]
    for c in x_copies:
        c.start()
    wait(sums)
    total = ar2[0]
    for o in range(1, ny):
        total = total + ar2[o]
    cells = 16.0 * 128.0 * nx * ny
    sum_f = jnp.sum(total[0:1, :], axis=1, keepdims=True)
    sum_m = jnp.sum(total[1:2, :], axis=1, keepdims=True)
    kappa = 0.8 * (sum_f / cells) / (S3 + 5.0 * (sum_m / cells))

    for x in range(8):
        v = base[x] + kappa * xk[4 + x, :, 4:12, :]
        pout[8 * x : 8 * x + 8, 0:128] = v[0]
        pout[8 * x : 8 * x + 8, 128:256] = v[1]
    wait(x_copies)
    for f in range(4):
        v = frecv[f] + kappa * fk[f]
        pout[64 + 8 * f : 72 + 8 * f, 0:128] = v[0]
        pout[64 + 8 * f : 72 + 8 * f, 128:256] = v[1]
    pout[...] = exact_dot(pout[:, 0:256], pmat[...])

    for j in range(8):
        for t in range(4):
            v = pout[8 * j : 8 * j + 8, 128 * t : 128 * t + 128]
            for q in range(2):
                for h in range(2):
                    rows = pl.ds(8 + h, 8, stride=2)
                    px[2 * j + 1 + q, t, rows, :] = px[2 * j + 1 + q, t, rows, :] + v
    for t in range(4):
        lanes = slice(128 * t, 128 * t + 128)
        for f in range(2):
            for h in range(2):
                rows = pl.ds(h, 8, stride=2)
                xr[1, f, t, rows, :] = xr[1, f, t, rows, :] + pout[64 + 8 * f : 72 + 8 * f, lanes]
                yr[1, f, t, rows, :] = yr[1, f, t, rows, :] + pout[80 + 8 * f : 88 + 8 * f, lanes]
    for f in range(2):
        d[15 * f] = d[15 * f] + kx[16 * f] * xr[1, f]
        dl[f] = kyf[f] * yr[1, f]
    add_rows(d, 0, 0)

    def fourth_sum(i):
        c, total = fine_sum(px, i)
        u[i + 1, :, IN, :] = w[i] * (d[i] + total) - INV * c

    planes(0, 16, 4, fourth_sum)
    pack_rows(u, 4)
    copies = fine_send(u, 4)

    def last_sum(i):
        c, total = fine_sum(u, i)
        g[i] = px[i + 1, :, IN, :] + (1.0 + ALPHA) * c + STEP * (w[i] * total)

    planes(0, 16, 4, last_sum)
    wait(copies)
    for f in range(2):
        g[15 * f] = g[15 * f] + gxf[f] * xr[4, f]
        dl[f] = gyf[f] * yr[4, f]
    add_rows(g, 0, 0)
    for i in range(16):
        for t in range(4):
            out[i, :, 128 * t : 128 * t + 128] = g[i, t]


def solution(mesh):
    nx, ny = mesh.shape["gx"], mesh.shape["gy"]

    def local(p, d, m):
        vm = lambda *s: pltpu.VMEM(s, F32)
        sem = lambda *s: pltpu.SemaphoreType.DMA(s)
        plane = (16, 4, 16, 128)
        face = (4, 16, 128)
        scratch = [
            vm(18, 4, 32, 128), vm(18, 4, 32, 128), vm(18, 4, 32, 128), vm(18, 4, 32, 128),
            vm(*plane), vm(*plane), vm(*plane), vm(*plane),
            vm(17, 4, 16, 128), vm(16, 4, 32, 128), vm(*plane),
            vm(5, 2, *face), vm(5, 2, *face), vm(5, 2, *face),
            vm(2, *face), vm(2, *face), vm(2, *face), vm(2, *face), vm(64, 512),
            pltpu.VMEM((512, 256), BF16), pltpu.VMEM((256, 512), BF16), vm(96, 512),
            vm(2, 8, 2, 8, 128), vm(2, 2, 4, 2, 8, 128), vm(2, 2, 4, 2, 8, 128),
            vm(2, 2, 4, 2, 8, 128), vm(2, 2, 2, 2, 2, 8, 128),
            vm(16, 2, 32, 128), vm(16, 2, 32, 128), vm(16, 2, 16, 128), vm(16, 2, 16, 128),
            vm(17, 2, 16, 128), vm(16, 2, 32, 128), vm(16, 2, 16, 128),
            vm(16, 2, 32, 128), vm(16, 2, 32, 128), vm(16, 2, 16, 128), vm(16, 2, 16, 128),
            vm(16, 2, 16, 128),
            vm(3, 16, 128), vm(3, 8, 16, 128), vm(12, 16, 128), vm(12, 16, 128), vm(12, 16, 128),
            vm(12, 16, 128), vm(6, 16, 128),
            vm(8, 2, 8, 128), vm(2, 2, 8, 128), vm(4, 2, 8, 128), vm(4, 2, 8, 128),
            vm(nx, 8, 128), vm(ny, 8, 128),
            sem(3, 4), sem(5, 4), sem(5, 4), sem(2, 8), sem(2, 8), sem(3, 8), sem(3, 8),
            sem(4), sem(4), sem(nx), sem(nx), sem(ny), sem(ny),
        ]
        return pl.pallas_call(
            functools.partial(kernel, nx, ny),
            out_shape=jax.ShapeDtypeStruct((16, 16, 512), F32),
            in_specs=[pl.BlockSpec(memory_space=pl.ANY)] * 3,
            out_specs=pl.BlockSpec(memory_space=pltpu.VMEM),
            scratch_shapes=scratch,
            compiler_params=pltpu.CompilerParams(
                collective_id=0, has_side_effects=True, vmem_limit_bytes=30 * 1024 * 1024
            ),
        )(*[pltpu.with_memory_space_constraint(a, pltpu.HBM) for a in (p, d, m)])

    spec = P("gx", "gy", None)
    return jax.shard_map(
        local, mesh=mesh, in_specs=(spec, spec, spec), out_specs=spec, check_vma=False
    )
```

time: 69 us -> 50.1 us (0.73)
  Pallas kernels: 66 us -> 48.6 us
  local copies, waits for them, and re-layouts: 1.88 us -> 0.8 us
    pallas_call x1, Pallas kernels: 66 us -> 48.6 us  [local(): pl.pallas_call(functools.partial(kernel, nx, ny), out_shape=jax.ShapeDtyp...]
    unnamed x1, local copies, waits for them, and re-layouts: 1.88 us -> 0.8 us
where the time goes in v1:
time: 50.1 us; the launch traced here: 49.4 us
  Pallas kernels  48.6 us (97%)
  local copies, waits for them, and re-layouts  0.8 us (2%)
    pallas_call x1, Pallas kernels, local(): pl.pallas_call(functools.partial(kernel, nx, ny), out_shape=jax.ShapeDtyp...  48.6 us

profile of v1, /device:TPU:1, one launch (start us, length us, event | category | flops | bytes accessed | tf_op | source)
XLA Modules:
  0.0 49.4 jit_solution(8822326512788297842)
XLA Ops:
  0.0 48.6 %shard_map.37 = f32[16,16,512]{2,1,0:T(8,128)S(1)} custom-call(f32[16,16,512]{2,1,0:T(8,128)} %p_hbm.1, f32[16,16,512]{2,1,0:T(8,128)} %d_hbm.1, f32[16,16,512]{2,1,0:T(8,128)} %m_hbm.1), custom_call_target="tpu_custom_call" | custom-call | tf_op jit(solution)/shard_map/pallas_call | solution.py:636
  48.6 0.8 %copy.5 = f32[16,16,512]{2,1,0:T(8,128)} copy(f32[16,16,512]{2,1,0:T(8,128)S(1)} %shard_map.37) | data formatting | bytes 1048576

commit v2 on v1

--- a/solution.py
+++ b/solution.py
@@ -93,6 +93,7 @@
     cstage, crecv, cm, cw, cb, ce, t2,
     base, fstage, frecv, fk,
     ar1, ar2,
+    cst, crn, vf, v2f, ktf, k12f, kzf, wf, uf, bcs, bcr,
     in_sem, fs, fr, ms, mr, cs, cr, xs, xrs, as1, ar1s, as2, ar2s,
 ):
     gx = lax.axis_index("gx")
@@ -164,15 +165,18 @@
     hit = (zi >> 1) == (((ci & 127) << 1) + (ci >> 7))
     pmat[...] = jnp.where(hit, 1.0, 0.0).astype(BF16)
 
-    def pack_rows(arr, n):
+    def pack_rows(arr, n, layer=0, off=1, row=8):
+        low, high = row + layer, row + 15 - layer
         for x in range(16):
-            ys[n, 0, :, x : x + 1, :] = arr[x + 1, :, 8:9, :]
-            ys[n, 1, :, x : x + 1, :] = arr[x + 1, :, 23:24, :]
-
-    def fine_send(arr, n):
+            ys[n, 0, :, x : x + 1, :] = arr[x + off, :, low : low + 1, :]
+            ys[n, 1, :, x : x + 1, :] = arr[x + off, :, high : high + 1, :]
+
+    def fine_send(arr, n, layer=0, off=1, row=8):
+        rows = slice(row, row + 16)
+        low, high = arr.at[off + layer, :, rows, :], arr.at[off + 15 - layer, :, rows, :]
         copies = [
-            remote(arr.at[1, :, IN, :], xr.at[n, 1], fs.at[n, 0], fr.at[n, 0], -1, 0),
-            remote(arr.at[16, :, IN, :], xr.at[n, 0], fs.at[n, 1], fr.at[n, 1], 1, 0),
+            remote(low, xr.at[n, 1], fs.at[n, 0], fr.at[n, 0], -1, 0),
+            remote(high, xr.at[n, 0], fs.at[n, 1], fr.at[n, 1], 1, 0),
             remote(ys.at[n, 0], yr.at[n, 1], fs.at[n, 2], fr.at[n, 2], 0, -1),
             remote(ys.at[n, 1], yr.at[n, 0], fs.at[n, 3], fr.at[n, 3], 0, 1),
         ]
@@ -183,6 +187,26 @@
     def wait(copies):
         for c in copies:
             c.wait()
+
+    def wait_sent(copies):
+        for c in copies:
+            c.wait_send()
+
+    def wait_arrived(copies):
+        for c in copies:
+            c.wait_recv()
+
+    def corner_send(arr, n):
+        copies = []
+        for k, (dx, dy) in enumerate(NEAR[4:]):
+            x, y = 1 + 15 * (k // 2), 8 + 15 * (k % 2)
+            for t in range(4):
+                cst[n, k, t : t + 1, :] = arr[x, t, y : y + 1, :]
+            copies.append(
+                remote(cst.at[n, k], crn.at[n, 3 - k], fs.at[7 + n, k], fr.at[7 + n, k], dx, dy)
+            )
+            copies[-1].start()
+        return copies
 
     def restrict_fine(arr, off, row, scale):
         for j in range(8):
@@ -311,7 +335,6 @@
     pl.semaphore_wait(barrier, len(peers))
     m_copies = fine_send(mf, 0)
     p_copies = fine_send(px, 1)
-    m2_copies = mid_send(0)
 
     def coefficients(i):
         c = mf[i + 1, :, IN, :]
@@ -334,8 +357,13 @@
         g[i] = d[i] + total
 
     planes(0, 16, 4, first_sum)
-
-    wait(m_copies)
+    pack_rows(d, 4, 0, 0, 0)
+    pack_rows(mf, 5, 1)
+    wait_sent(m_copies)
+    wait_sent(p_copies)
+    m2_copies = mid_send(0)
+
+    wait_arrived(m_copies)
     for f in range(2):
         face = 0.5 * xr[0, f]
         kx[16 * f] = kx[16 * f] + face
@@ -344,7 +372,7 @@
         kyf[f] = 0.5 * ys[0, f] + face
         dl[f] = face
     add_rows(dg, 0, 0)
-    wait(p_copies)
+    wait_arrived(p_copies)
     for f in range(2):
         g[15 * f] = g[15 * f] + kx[16 * f] * xr[1, f]
         dl[f] = kyf[f] * yr[1, f]
@@ -375,8 +403,10 @@
     mid_place(0, m2)
     coarse_block(m2, 0, 12, 0.125)
     m3_copies = coarse_send(0)
-
-    wait(u_copies)
+    wait_sent(u_copies)
+    d_copies = fine_send(d, 4, 0, 0, 0)
+
+    wait_arrived(u_copies)
     for f in range(2):
         k = 1 + 15 * f
         u2[k, :, IN, :] = u2[k, :, IN, :] + gxf[f] * xr[2, f]
@@ -417,8 +447,10 @@
     for x in range(4):
         cstage[1, 4 * x : 4 * x + 4, :] = cw[4 + x, 4:8, :]
     w3_copies = coarse_send(1)
-
-    wait(u2_copies)
+    wait_sent(u2_copies)
+    far_copies = fine_send(mf, 5, 1) + corner_send(mf, 0)
+
+    wait_arrived(u2_copies)
     for f in range(2):
         g[15 * f] = g[15 * f] + kx[16 * f] * xr[3, f]
         dl[f] = kyf[f] * yr[3, f]
@@ -426,6 +458,7 @@
     mid_put(1, restrict_fine(g, 0, 0, 0.5))
     b2_copies = mid_send(1)
 
+    pack_rows(px, 6, 1)
     def response_one(i):
         vb[i, :, IN, :] = (-S2) * w2[i]
 
@@ -454,7 +487,9 @@
         xr[1, f] = xr[1, f] + xr[2, f] + xr[3, f]
         yr[1, f] = yr[1, f] + yr[2, f] + yr[3, f]
     mid_own(1, b2)
-    wait(b2_copies)
+    wait_sent(b2_copies)
+    x1_copies = fine_send(px, 6, 1) + corner_send(px, 1)
+    wait_arrived(b2_copies)
     mid_place(1, b2)
 
     def mid_one(i):
@@ -485,12 +520,36 @@
             ce[x, 4:8, :] * cstage[2, 4 * x : 4 * x + 4, :], axis=0, keepdims=True
         )
         partm = partm + jnp.sum(cstage[0, 4 * x : 4 * x + 4, :], axis=0, keepdims=True)
-    row = lax.broadcasted_iota(jnp.int32, (8, 128), 0)
-    ar1[0] = jnp.where(row < 1, part, partm)
+    ar1[0, 0:1, :] = part
+    ar1[0, 1:2, :] = partm
     sums = []
     for o in range(1, nx):
         sums.append(remote(ar1.at[0], ar1.at[o], as1.at[o], ar1s.at[o], o, 0))
         sums[-1].start()
+
+    wait(d_copies)
+    wait(far_copies)
+
+    def corners(f):
+        return ((0, 1), (2, 3), (0, 2), (1, 3))[f]
+
+    for f in range(4):
+        first, second = (xr.at[0, f], xr.at[5, f]) if f < 2 else (yr.at[0, f - 2], yr.at[5, f - 2])
+        k01 = kx[16 * f] if f < 2 else kyf[f - 2]
+        c = first[...]
+        vf[f, :, IN, :] = c
+        for row, k in zip((7, 24), corners(f)):
+            for t in range(4):
+                vf[f, t, row : row + 1, :] = crn[0, k, t : t + 1, :]
+        ktf[f, :, IN, :] = 0.5 * (c + vf[f, :, HI, :])
+        ktf[f, :, 7:8, :] = 0.5 * (vf[f, :, 7:8, :] + vf[f, :, 8:9, :])
+        k12 = 0.5 * (c + second[...])
+        after = 0.5 * (c + fine_next(c))
+        k12f[f] = k12
+        kzf[f] = after
+        wf[f] = INV / (
+            S1 + k01 + k12 + ktf[f, :, IN, :] + ktf[f, :, LO, :] + after + fine_before(after)
+        )
 
     coarse_wait(b3_copies, 2, cb)
     rhs = cb[...]
@@ -541,8 +600,16 @@
         remote(fstage.at[0], frecv.at[3], xs.at[2], xrs.at[2], 0, -1),
         remote(fstage.at[1], frecv.at[2], xs.at[3], xrs.at[3], 0, 1),
     ]
+    for k, (dx, dy) in enumerate(NEAR[4:]):
+        x, y = 7 * (k // 2), 7 * (k % 2)
+        for t in range(2):
+            bcs[k, t : t + 1, :] = base[x, t, y : y + 1, :]
+        x_copies.append(
+            remote(bcs.at[k], bcr.at[3 - k], xs.at[4 + k], xrs.at[4 + k], dx, dy)
+        )
     for c in x_copies:
         c.start()
+    wait(x1_copies)
     wait(sums)
     total = ar2[0]
     for o in range(1, ny):
@@ -561,6 +628,12 @@
         v = frecv[f] + kappa * fk[f]
         pout[64 + 8 * f : 72 + 8 * f, 0:128] = v[0]
         pout[64 + 8 * f : 72 + 8 * f, 128:256] = v[1]
+    for k in range(4):
+        x, y = 3 + 9 * (k // 2), 3 + 9 * (k % 2)
+        for t in range(2):
+            pout[96 + k : 97 + k, 128 * t : 128 * t + 128] = (
+                bcr[k, t : t + 1, :] + kappa * xk[x, t, y : y + 1, :]
+            )
     pout[...] = exact_dot(pout[:, 0:256], pmat[...])
 
     for j in range(8):
@@ -570,35 +643,49 @@
                 for h in range(2):
                     rows = pl.ds(8 + h, 8, stride=2)
                     px[2 * j + 1 + q, t, rows, :] = px[2 * j + 1 + q, t, rows, :] + v
-    for t in range(4):
-        lanes = slice(128 * t, 128 * t + 128)
-        for f in range(2):
+    for f in range(4):
+        first, second = (xr.at[1, f], xr.at[6, f]) if f < 2 else (yr.at[1, f - 2], yr.at[6, f - 2])
+        for t in range(4):
+            lanes = slice(128 * t, 128 * t + 128)
+            v = pout[64 + 8 * f : 72 + 8 * f, lanes]
             for h in range(2):
                 rows = pl.ds(h, 8, stride=2)
-                xr[1, f, t, rows, :] = xr[1, f, t, rows, :] + pout[64 + 8 * f : 72 + 8 * f, lanes]
-                yr[1, f, t, rows, :] = yr[1, f, t, rows, :] + pout[80 + 8 * f : 88 + 8 * f, lanes]
+                vf[f, t, pl.ds(8 + h, 8, stride=2), :] = first[t, rows, :] + v
+                v2f[f, t, rows, :] = second[t, rows, :] + v
+            for row, k in zip((7, 24), corners(f)):
+                vf[f, t, row : row + 1, :] = crn[1, k, t : t + 1, :] + pout[96 + k : 97 + k, lanes]
+    pack_rows(px, 1)
     for f in range(2):
-        d[15 * f] = d[15 * f] + kx[16 * f] * xr[1, f]
-        dl[f] = kyf[f] * yr[1, f]
+        d[15 * f] = d[15 * f] + kx[16 * f] * vf[f, :, IN, :]
+        dl[f] = kyf[f] * vf[2 + f, :, IN, :]
     add_rows(d, 0, 0)
+
+    for f in range(4):
+        if f < 2:
+            k01, inside, rhs_f = kx[16 * f], px[1 + 15 * f, :, IN, :], xr[4, f]
+        else:
+            k01, inside, rhs_f = kyf[f - 2], ys[1, f - 2], yr[4, f - 2]
+        c = vf[f, :, IN, :]
+        z = kzf[f]
+        total = k01 * inside + k12f[f] * v2f[f]
+        total = total + ktf[f, :, LO, :] * vf[f, :, LO, :] + ktf[f, :, IN, :] * vf[f, :, HI, :]
+        total = total + z * fine_next(c) + fine_before(z * c)
+        uf[f] = wf[f] * (rhs_f + total) - INV * c
 
     def fourth_sum(i):
         c, total = fine_sum(px, i)
         u[i + 1, :, IN, :] = w[i] * (d[i] + total) - INV * c
 
     planes(0, 16, 4, fourth_sum)
-    pack_rows(u, 4)
-    copies = fine_send(u, 4)
 
     def last_sum(i):
         c, total = fine_sum(u, i)
         g[i] = px[i + 1, :, IN, :] + (1.0 + ALPHA) * c + STEP * (w[i] * total)
 
     planes(0, 16, 4, last_sum)
-    wait(copies)
     for f in range(2):
-        g[15 * f] = g[15 * f] + gxf[f] * xr[4, f]
-        dl[f] = gyf[f] * yr[4, f]
+        g[15 * f] = g[15 * f] + gxf[f] * uf[f]
+        dl[f] = gyf[f] * uf[2 + f]
     add_rows(g, 0, 0)
     for i in range(16):
         for t in range(4):
@@ -617,9 +704,9 @@
             vm(18, 4, 32, 128), vm(18, 4, 32, 128), vm(18, 4, 32, 128), vm(18, 4, 32, 128),
             vm(*plane), vm(*plane), vm(*plane), vm(*plane),
             vm(17, 4, 16, 128), vm(16, 4, 32, 128), vm(*plane),
-            vm(5, 2, *face), vm(5, 2, *face), vm(5, 2, *face),
+            vm(7, 2, *face), vm(7, 2, *face), vm(7, 2, *face),
             vm(2, *face), vm(2, *face), vm(2, *face), vm(2, *face), vm(64, 512),
-            pltpu.VMEM((512, 256), BF16), pltpu.VMEM((256, 512), BF16), vm(96, 512),
+            pltpu.VMEM((512, 256), BF16), pltpu.VMEM((256, 512), BF16), vm(104, 512),
             vm(2, 8, 2, 8, 128), vm(2, 2, 4, 2, 8, 128), vm(2, 2, 4, 2, 8, 128),
             vm(2, 2, 4, 2, 8, 128), vm(2, 2, 2, 2, 2, 8, 128),
             vm(16, 2, 32, 128), vm(16, 2, 32, 128), vm(16, 2, 16, 128), vm(16, 2, 16, 128),
@@ -629,9 +716,11 @@
             vm(3, 16, 128), vm(3, 8, 16, 128), vm(12, 16, 128), vm(12, 16, 128), vm(12, 16, 128),
             vm(12, 16, 128), vm(6, 16, 128),
             vm(8, 2, 8, 128), vm(2, 2, 8, 128), vm(4, 2, 8, 128), vm(4, 2, 8, 128),
-            vm(nx, 8, 128), vm(ny, 8, 128),
-            sem(3, 4), sem(5, 4), sem(5, 4), sem(2, 8), sem(2, 8), sem(3, 8), sem(3, 8),
-            sem(4), sem(4), sem(nx), sem(nx), sem(ny), sem(ny),
+            vm(nx, 2, 128), vm(ny, 2, 128),
+            vm(2, 4, 4, 128), vm(2, 4, 4, 128), vm(4, 4, 32, 128), vm(4, *face), vm(4, 4, 32, 128),
+            vm(4, *face), vm(4, *face), vm(4, *face), vm(4, *face), vm(4, 2, 128), vm(4, 2, 128),
+            sem(3, 4), sem(9, 4), sem(9, 4), sem(2, 8), sem(2, 8), sem(3, 8), sem(3, 8),
+            sem(8), sem(8), sem(nx), sem(nx), sem(ny), sem(ny),
         ]
         return pl.pallas_call(
             functools.partial(kernel, nx, ny),

time: 50.1 us -> 48.3 us (0.964)
  Pallas kernels: 48.6 us -> 47.2 us
    pallas_call x1, Pallas kernels: 48.6 us -> 47.2 us  [local(): pl.pallas_call(functools.partial(kernel, nx, ny), out_shape=jax.ShapeDtyp...]
where the time goes in v2:
time: 48.3 us; the launch traced here: 48 us
  Pallas kernels  47.2 us (98%)
  local copies, waits for them, and re-layouts  0.8 us (2%)
    pallas_call x1, Pallas kernels, local(): pl.pallas_call(functools.partial(kernel, nx, ny), out_shape=jax.ShapeDtyp...  47.2 us

profile of v2, /device:TPU:1, one launch (start us, length us, event | category | flops | bytes accessed | tf_op | source)
XLA Modules:
  0.0 48.0 jit_solution(5906762560741068797)
XLA Ops:
  0.0 47.2 %shard_map.37 = f32[16,16,512]{2,1,0:T(8,128)S(1)} custom-call(f32[16,16,512]{2,1,0:T(8,128)} %p_hbm.1, f32[16,16,512]{2,1,0:T(8,128)} %d_hbm.1, f32[16,16,512]{2,1,0:T(8,128)} %m_hbm.1), custom_call_target="tpu_custom_call" | custom-call | tf_op jit(solution)/shard_map/pallas_call | solution.py:725
  47.2 0.8 %copy.5 = f32[16,16,512]{2,1,0:T(8,128)} copy(f32[16,16,512]{2,1,0:T(8,128)S(1)} %shard_map.37) | data formatting | bytes 1048576

commit v3 on v2

--- a/solution.py
+++ b/solution.py
@@ -26,6 +26,7 @@
 STEP = CB * MIDPOINT
 BETA = 1.0 / CB - 1.0
 GAMMA = CA / CB
+FAR = [(x, y) for x in range(-2, 3) for y in range(-2, 3) if max(abs(x), abs(y)) == 2]
 NEAR = [(-1, 0), (1, 0), (0, -1), (0, 1), (-1, -1), (-1, 1), (1, -1), (1, 1)]
 
 
@@ -89,12 +90,12 @@
     px, mf, u, u2, d, g, dg, w, kx, ky, kz,
     xr, ys, yr, kyf, gyf, gxf, dl, rs, tmat, pmat, pout,
     mid_b, mid_stage, mid_rx, mid_ry, mid_rc, b2, m2, w2, d2, kx2, ky2, kz2,
-    va, vb, rr, x2, xk,
+    va, vb, rr, x2,
     cstage, crecv, cm, cw, cb, ce, t2,
-    base, fstage, frecv, fk,
+    base, cedge, cfar,
     ar1, ar2,
-    cst, crn, vf, v2f, ktf, k12f, kzf, wf, uf, bcs, bcr,
-    in_sem, fs, fr, ms, mr, cs, cr, xs, xrs, as1, ar1s, as2, ar2s,
+    cst, crn, vf, v2f, ktf, k12f, kzf, wf, uf,
+    in_sem, fs, fr, ms, mr, cs, cr, as1, ar1s, as2, ar2s,
 ):
     gx = lax.axis_index("gx")
     gy = lax.axis_index("gy")
@@ -106,7 +107,7 @@
         return (lax.rem(gx + (ox % nx), nx), lax.rem(gy + (oy % ny), ny))
 
     peers = {(o, 0) for o in range(1, nx)} | {(0, o) for o in range(1, ny)}
-    peers |= {(dx % nx, dy % ny) for dx, dy in NEAR}
+    peers |= {(dx % nx, dy % ny) for dx, dy in NEAR + FAR}
     peers = sorted(peers - {(0, 0)})
 
     loads = []
@@ -220,13 +221,16 @@
         return exact_dot(rs[...], tmat[...])
 
     def mid_put(n, got):
-        low = lax.broadcasted_iota(jnp.int32, (2, 8, 128), 1) < 4
         blocks = []
         for x in range(8):
             rows = got[8 * x : 8 * x + 8]
             v = jnp.stack([rows[:, :128], rows[:, 128:]], axis=0)
             mid_b[n, x] = v
             blocks.append(v)
+        mid_fold(n, blocks)
+
+    def mid_fold(n, blocks):
+        low = lax.broadcasted_iota(jnp.int32, (2, 8, 128), 1) < 4
         for t in range(4):
             a, b = blocks[2 * t], blocks[2 * t + 1]
             mid_stage[n, 0, t] = jnp.where(low, a, pltpu.roll(b, 4, 1))
@@ -284,23 +288,52 @@
             cstage[n, 4 * x : 4 * x + 4, :] = total * scale
 
     def coarse_send(n):
+        cedge[n, 0] = cstage[n, 0:4, :]
+        cedge[n, 1] = cstage[n, 12:16, :]
+        for x in range(4):
+            for k in range(2):
+                cedge[n, 2 + k, x : x + 1, :] = cstage[n, 4 * x + 3 * k : 4 * x + 3 * k + 1, :]
         copies = []
         for k, (dx, dy) in enumerate(NEAR):
             copies.append(
                 remote(cstage.at[n], crecv.at[n, k], cs.at[n, k], cr.at[n, k], dx, dy)
             )
             copies[-1].start()
+        for k, (dx, dy) in enumerate(FAR):
+            side = (dx == 2) if abs(dx) == 2 else 2 + (dy == 2)
+            copies.append(
+                remote(
+                    cedge.at[n, int(side)], cfar.at[n, k],
+                    cs.at[n, 8 + k], cr.at[n, 8 + k], dx, dy,
+                )
+            )
+            copies[-1].start()
         return copies
 
-    def coarse_wait(copies, n, ext):
+    def coarse_wait(copies, n, ext, sent=True):
         def place(dx, dy, block):
             for x in range(4):
-                ext[4 * dx + 4 + x, 4 * dy + 4 : 4 * dy + 8, :] = block[4 * x : 4 * x + 4, :]
+                ext[4 * dx + 5 + x, 4 * dy + 5 : 4 * dy + 9, :] = block[4 * x : 4 * x + 4, :]
 
         place(0, 0, cstage.at[n])
-        wait(copies)
+        if sent:
+            wait_sent(copies)
+        wait_arrived(copies)
         for k, (dx, dy) in enumerate(NEAR):
             place(-dx, -dy, crecv.at[n, k])
+        for k, (dx, dy) in enumerate(FAR):
+            far = cfar.at[n, k]
+            if abs(dx) == 2:
+                plane = 0 if dx == 2 else 13
+                if abs(dy) == 2:
+                    row, at = (0, 3) if dy == 2 else (13, 0)
+                    ext[plane, row : row + 1, :] = far[at : at + 1, :]
+                else:
+                    ext[plane, 5 - 4 * dy : 9 - 4 * dy, :] = far[...]
+            else:
+                row = 0 if dy == 2 else 13
+                for x in range(4):
+                    ext[5 - 4 * dx + x, row : row + 1, :] = far[x : x + 1, :]
 
     def fine_sum(arr, i):
         c = arr[i + 1, :, IN, :]
@@ -437,18 +470,21 @@
         kz2[i] = after
         diagonal = (S2 + below + above + right + after) + 0.5 * (left + before)
         d2[i] = diagonal
-        w2[i] = INV / diagonal
+        w2[i, :, IN, :] = INV / diagonal
 
     planes(1, 15, 7, mid_coefficients)
     coarse_wait(m3_copies, 0, cm)
     mob = cm[...]
     lap = weighted_sum(mob)
-    cw[1:11] = 0.8 / (S3 + 0.5 * (5.0 * mob[1:-1] + lap))
+    cw[1:13] = 0.8 / (S3 + 0.5 * (5.0 * mob[1:-1] + lap))
     for x in range(4):
-        cstage[1, 4 * x : 4 * x + 4, :] = cw[4 + x, 4:8, :]
+        cstage[1, 4 * x : 4 * x + 4, :] = cw[5 + x, 5:9, :]
     w3_copies = coarse_send(1)
+    for x in range(8):
+        mid_b[2, x] = w2[4 + x, :, 12:20, :]
+    mid_fold(2, [mid_b[2, x] for x in range(8)])
     wait_sent(u2_copies)
-    far_copies = fine_send(mf, 5, 1) + corner_send(mf, 0)
+    w2_copies = mid_send(2)
 
     wait_arrived(u2_copies)
     for f in range(2):
@@ -459,51 +495,77 @@
     b2_copies = mid_send(1)
 
     pack_rows(px, 6, 1)
-    def response_one(i):
-        vb[i, :, IN, :] = (-S2) * w2[i]
-
-    planes(1, 15, 7, response_one)
-
-    def response_two(i):
-        c, total = mid_sum(vb, i)
-        xk[i] = 1.0 + (1.0 + ALPHA) * c + STEP * (w2[i] * total)
-
-    planes(2, 14, 6, response_two)
-    for x in range(8):
-        fk[2, :, x : x + 1, :] = xk[4 + x, :, 3:4, :]
-        fk[3, :, x : x + 1, :] = xk[4 + x, :, 12:13, :]
-    fk[0] = xk[3, :, 4:12, :]
-    fk[1] = xk[12, :, 4:12, :]
     coarse_wait(w3_copies, 1, cw)
     weight = cw[...]
     y = jnp.ones_like(weight)
     psi = y
     for k in range(3):
-        inner = slice(k, 12 - k)
-        y = y[1:-1] - coarse_operator(weight[inner] * y, mob[inner], lap[k : 10 - k])
+        inner = slice(k, 14 - k)
+        y = y[1:-1] - coarse_operator(weight[inner] * y, mob[inner], lap[k : 12 - k])
         psi = psi[1:-1] + y
-    ce[0:4] = 1.0 - S3 * (weight[4:8] * psi[1:5])
+    ce[3:11] = 0.5 - (0.5 * S3) * (weight[3:11] * psi)
+
+    def double_rows():
+        for x in range(8):
+            for h in range(2):
+                t2[x, pl.ds(h, 8, stride=2), :] = ce[3 + x, 3:11, :]
+
+    def double(x):
+        v = t2[x]
+        return jnp.stack([v, v], axis=0)
+
+    double_rows()
+    for x in range(8):
+        v = double(x)
+        for q in range(2):
+            va[2 * x + q, :, IN, :] = v
+
+    def adjoint_one(i):
+        c, total = mid_sum(va, i)
+        vb[i, :, IN, :] = w2[i, :, IN, :] * (d2[i] * c - total)
+
+    planes(3, 13, 5, adjoint_one)
+
+    def adjoint_two(i):
+        c, total = mid_sum(vb, i)
+        x2[i] = va[i, :, IN, :] - (1.0 + ALPHA) * c - STEP * (w2[i, :, IN, :] * total)
+
+    planes(4, 12, 4, adjoint_two)
+    part = jnp.zeros((2, 8, 128), F32)
+    for x in range(8):
+        part = part + x2[4 + x, :, 4:12, :] * mid_b[1, x]
+    partm = jnp.zeros((4, 128), F32)
+    for x in range(4):
+        partm = partm + cstage[0, 4 * x : 4 * x + 4, :]
+    ar1[0, 0:1, :] = jnp.sum(part[0] + part[1], axis=0, keepdims=True)
+    ar1[0, 1:2, :] = jnp.sum(partm, axis=0, keepdims=True)
+    wait_sent(b2_copies)
+    sums = []
+    for o in range(1, nx):
+        sums.append(remote(ar1.at[0], ar1.at[o], as1.at[o], ar1s.at[o], o, 0))
+        sums[-1].start()
+    far_copies = fine_send(mf, 5, 1) + corner_send(mf, 0)
+    wait(w2_copies)
+    mid_place(2, w2)
     for f in range(2):
         xr[1, f] = xr[1, f] + xr[2, f] + xr[3, f]
         yr[1, f] = yr[1, f] + yr[2, f] + yr[3, f]
     mid_own(1, b2)
-    wait_sent(b2_copies)
-    x1_copies = fine_send(px, 6, 1) + corner_send(px, 1)
     wait_arrived(b2_copies)
     mid_place(1, b2)
 
     def mid_one(i):
-        va[i, :, IN, :] = w2[i] * b2[i, :, IN, :]
-
-    planes(1, 15, 7, mid_one)
+        va[i, :, IN, :] = w2[i, :, IN, :] * b2[i, :, IN, :]
+
+    planes(0, 16, 8, mid_one)
 
     def mid_two(i):
         c, total = mid_sum(va, i)
-        step = ALPHA * c + STEP * (w2[i] * total)
+        step = ALPHA * c + STEP * (w2[i, :, IN, :] * total)
         vb[i, :, IN, :] = step
         x2[i] = c + step
 
-    planes(2, 14, 6, mid_two)
+    planes(1, 15, 7, mid_two)
 
     def mid_three(i):
         c, total = mid_sum(vb, i)
@@ -513,19 +575,17 @@
     coarse_block(rr, 2, 4, 0.5)
     b3_copies = coarse_send(2)
 
-    part = jnp.zeros((1, 128), F32)
-    partm = jnp.zeros((1, 128), F32)
-    for x in range(4):
-        part = part + jnp.sum(
-            ce[x, 4:8, :] * cstage[2, 4 * x : 4 * x + 4, :], axis=0, keepdims=True
-        )
-        partm = partm + jnp.sum(cstage[0, 4 * x : 4 * x + 4, :], axis=0, keepdims=True)
-    ar1[0, 0:1, :] = part
-    ar1[0, 1:2, :] = partm
+    wait(sums)
+    total = ar1[0]
+    for o in range(1, nx):
+        total = total + ar1[o]
+    ar2[0] = total
     sums = []
-    for o in range(1, nx):
-        sums.append(remote(ar1.at[0], ar1.at[o], as1.at[o], ar1s.at[o], o, 0))
+    for o in range(1, ny):
+        sums.append(remote(ar2.at[0], ar2.at[o], as2.at[o], ar2s.at[o], 0, o))
         sums[-1].start()
+    wait_sent(b3_copies)
+    x1_copies = fine_send(px, 6, 1) + corner_send(px, 1)
 
     wait(d_copies)
     wait(far_copies)
@@ -551,65 +611,14 @@
             S1 + k01 + k12 + ktf[f, :, IN, :] + ktf[f, :, LO, :] + after + fine_before(after)
         )
 
-    coarse_wait(b3_copies, 2, cb)
+    coarse_wait(b3_copies, 2, cb, False)
     rhs = cb[...]
     e = weight * rhs
     for k in range(3):
-        inner = slice(k, 12 - k)
-        e = e[1:-1] + weight[k + 1 : 11 - k] * (
-            rhs[k + 1 : 11 - k] - coarse_operator(e, mob[inner], lap[k : 10 - k])
+        inner = slice(k, 14 - k)
+        e = e[1:-1] + weight[k + 1 : 13 - k] * (
+            rhs[k + 1 : 13 - k] - coarse_operator(e, mob[inner], lap[k : 12 - k])
         )
-    wait(sums)
-    total = ar1[0]
-    for o in range(1, nx):
-        total = total + ar1[o]
-    ar2[0] = total
-    sums = []
-    for o in range(1, ny):
-        sums.append(remote(ar2.at[0], ar2.at[o], as2.at[o], ar2s.at[o], 0, o))
-        sums[-1].start()
-
-    ce[3:9] = e
-    for x in range(6):
-        for h in range(2):
-            t2[x, pl.ds(h, 8, stride=2), :] = ce[3 + x, 2:10, :]
-    for x in range(6):
-        v = t2[x]
-        both = jnp.stack([v, v], axis=0)
-        for q in range(2):
-            va[2 + 2 * x + q, :, IN, :] = x2[2 + 2 * x + q] + both
-
-    def post_one(i):
-        c, total = mid_sum(va, i)
-        vb[i, :, IN, :] = w2[i] * (b2[i, :, IN, :] + total) - INV * c
-
-    planes(3, 13, 5, post_one)
-
-    def post_two(i):
-        c, total = mid_sum(vb, i)
-        done = va[i, :, IN, :] + (1.0 + ALPHA) * c + STEP * (w2[i] * total)
-        base[i - 4] = done[:, 4:12, :]
-
-    planes(4, 12, 4, post_two)
-    for x in range(8):
-        fstage[0, :, x : x + 1, :] = base[x, :, 0:1, :]
-        fstage[1, :, x : x + 1, :] = base[x, :, 7:8, :]
-    x_copies = [
-        remote(base.at[0], frecv.at[1], xs.at[0], xrs.at[0], -1, 0),
-        remote(base.at[7], frecv.at[0], xs.at[1], xrs.at[1], 1, 0),
-        remote(fstage.at[0], frecv.at[3], xs.at[2], xrs.at[2], 0, -1),
-        remote(fstage.at[1], frecv.at[2], xs.at[3], xrs.at[3], 0, 1),
-    ]
-    for k, (dx, dy) in enumerate(NEAR[4:]):
-        x, y = 7 * (k // 2), 7 * (k % 2)
-        for t in range(2):
-            bcs[k, t : t + 1, :] = base[x, t, y : y + 1, :]
-        x_copies.append(
-            remote(bcs.at[k], bcr.at[3 - k], xs.at[4 + k], xrs.at[4 + k], dx, dy)
-        )
-    for c in x_copies:
-        c.start()
-    wait(x1_copies)
     wait(sums)
     total = ar2[0]
     for o in range(1, ny):
@@ -619,22 +628,41 @@
     sum_m = jnp.sum(total[1:2, :], axis=1, keepdims=True)
     kappa = 0.8 * (sum_f / cells) / (S3 + 5.0 * (sum_m / cells))
 
+    ce[3:11] = e + kappa
+    double_rows()
     for x in range(8):
-        v = base[x] + kappa * xk[4 + x, :, 4:12, :]
-        pout[8 * x : 8 * x + 8, 0:128] = v[0]
-        pout[8 * x : 8 * x + 8, 128:256] = v[1]
-    wait(x_copies)
-    for f in range(4):
-        v = frecv[f] + kappa * fk[f]
-        pout[64 + 8 * f : 72 + 8 * f, 0:128] = v[0]
-        pout[64 + 8 * f : 72 + 8 * f, 128:256] = v[1]
-    for k in range(4):
-        x, y = 3 + 9 * (k // 2), 3 + 9 * (k % 2)
-        for t in range(2):
-            pout[96 + k : 97 + k, 128 * t : 128 * t + 128] = (
-                bcr[k, t : t + 1, :] + kappa * xk[x, t, y : y + 1, :]
-            )
+        v = double(x)
+        for q in range(2):
+            if 0 < 2 * x + q < 15:
+                va[2 * x + q, :, IN, :] = x2[2 * x + q] + v
+
+    def post_one(i):
+        c, total = mid_sum(va, i)
+        vb[i, :, IN, :] = w2[i, :, IN, :] * (b2[i, :, IN, :] + total) - INV * c
+
+    planes(2, 14, 6, post_one)
+
+    def post_two(i):
+        c, total = mid_sum(vb, i)
+        base[i - 3] = (
+            va[i, :, IN, :] + (1.0 + ALPHA) * c + STEP * (w2[i, :, IN, :] * total)
+        )
+
+    planes(3, 13, 5, post_two)
+    for t in range(2):
+        lanes = slice(128 * t, 128 * t + 128)
+        for x in range(8):
+            pout[8 * x : 8 * x + 8, lanes] = base[1 + x, t, 4:12, :]
+            for f in range(2):
+                row = 3 + 9 * f
+                pout[80 + 8 * f + x : 81 + 8 * f + x, lanes] = base[1 + x, t, row : row + 1, :]
+        for f in range(2):
+            pout[64 + 8 * f : 72 + 8 * f, lanes] = base[9 * f, t, 4:12, :]
+        for k in range(4):
+            row = 3 + 9 * (k % 2)
+            pout[96 + k : 97 + k, lanes] = base[9 * (k // 2), t, row : row + 1, :]
     pout[...] = exact_dot(pout[:, 0:256], pmat[...])
+    wait(x1_copies)
 
     for j in range(8):
         for t in range(4):
@@ -707,20 +735,19 @@
             vm(7, 2, *face), vm(7, 2, *face), vm(7, 2, *face),
             vm(2, *face), vm(2, *face), vm(2, *face), vm(2, *face), vm(64, 512),
             pltpu.VMEM((512, 256), BF16), pltpu.VMEM((256, 512), BF16), vm(104, 512),
-            vm(2, 8, 2, 8, 128), vm(2, 2, 4, 2, 8, 128), vm(2, 2, 4, 2, 8, 128),
-            vm(2, 2, 4, 2, 8, 128), vm(2, 2, 2, 2, 2, 8, 128),
-            vm(16, 2, 32, 128), vm(16, 2, 32, 128), vm(16, 2, 16, 128), vm(16, 2, 16, 128),
+            vm(3, 8, 2, 8, 128), vm(3, 2, 4, 2, 8, 128), vm(3, 2, 4, 2, 8, 128),
+            vm(3, 2, 4, 2, 8, 128), vm(3, 2, 2, 2, 2, 8, 128),
+            vm(16, 2, 32, 128), vm(16, 2, 32, 128), vm(16, 2, 32, 128), vm(16, 2, 16, 128),
             vm(17, 2, 16, 128), vm(16, 2, 32, 128), vm(16, 2, 16, 128),
             vm(16, 2, 32, 128), vm(16, 2, 32, 128), vm(16, 2, 16, 128), vm(16, 2, 16, 128),
-            vm(16, 2, 16, 128),
-            vm(3, 16, 128), vm(3, 8, 16, 128), vm(12, 16, 128), vm(12, 16, 128), vm(12, 16, 128),
-            vm(12, 16, 128), vm(6, 16, 128),
-            vm(8, 2, 8, 128), vm(2, 2, 8, 128), vm(4, 2, 8, 128), vm(4, 2, 8, 128),
+            vm(3, 16, 128), vm(3, 8, 16, 128), vm(14, 16, 128), vm(14, 16, 128), vm(14, 16, 128),
+            vm(14, 16, 128), vm(8, 16, 128),
+            vm(10, 2, 16, 128), vm(3, 4, 4, 128), vm(3, 16, 4, 128),
             vm(nx, 2, 128), vm(ny, 2, 128),
             vm(2, 4, 4, 128), vm(2, 4, 4, 128), vm(4, 4, 32, 128), vm(4, *face), vm(4, 4, 32, 128),
-            vm(4, *face), vm(4, *face), vm(4, *face), vm(4, *face), vm(4, 2, 128), vm(4, 2, 128),
-            sem(3, 4), sem(9, 4), sem(9, 4), sem(2, 8), sem(2, 8), sem(3, 8), sem(3, 8),
-            sem(8), sem(8), sem(nx), sem(nx), sem(ny), sem(ny),
+            vm(4, *face), vm(4, *face), vm(4, *face), vm(4, *face),
+            sem(3, 4), sem(9, 4), sem(9, 4), sem(3, 8), sem(3, 8), sem(3, 24), sem(3, 24),
+            sem(nx), sem(nx), sem(ny), sem(ny),
         ]
         return pl.pallas_call(
             functools.partial(kernel, nx, ny),

time: 48.3 us -> 49.5 us (1.025)
  Pallas kernels: 47.2 us -> 48.5 us
    pallas_call x1, Pallas kernels: 47.2 us -> 48.5 us  [local(): pl.pallas_call(functools.partial(kernel, nx, ny), out_shape=jax.ShapeDtyp...]
where the time goes in v3:
time: 49.5 us; the launch traced here: 49.4 us
  Pallas kernels  48.5 us (98%)
  local copies, waits for them, and re-layouts  0.8 us (2%)
    pallas_call x1, Pallas kernels, local(): pl.pallas_call(functools.partial(kernel, nx, ny), out_shape=jax.ShapeDtyp...  48.5 us

profile of v3, /device:TPU:1, one launch (start us, length us, event | category | flops | bytes accessed | tf_op | source)
XLA Modules:
  0.0 49.4 jit_solution(11728767219923122653)
XLA Ops:
  0.0 48.5 %shard_map.37 = f32[16,16,512]{2,1,0:T(8,128)S(1)} custom-call(f32[16,16,512]{2,1,0:T(8,128)} %p_hbm.1, f32[16,16,512]{2,1,0:T(8,128)} %d_hbm.1, f32[16,16,512]{2,1,0:T(8,128)} %m_hbm.1), custom_call_target="tpu_custom_call" | custom-call | tf_op jit(solution)/shard_map/pallas_call | solution.py:752
  48.6 0.8 %copy.5 = f32[16,16,512]{2,1,0:T(8,128)} copy(f32[16,16,512]{2,1,0:T(8,128)S(1)} %shard_map.37) | data formatting | bytes 1048576

commit v4 on v3

--- a/solution.py
+++ b/solution.py
@@ -277,28 +277,28 @@
         for x in range(8):
             ext[4 + x, :, 12:20, :] = mid_b[n, x]
 
-    def coarse_block(arr, n, row, scale):
+    def coarse_block(arr, n, first, row, scale):
         for x in range(4):
             total = None
             for q in range(2):
                 for t in range(2):
                     for h in range(2):
-                        part = arr[4 + 2 * x + q, t, pl.ds(row + h, 4, stride=2), :]
+                        part = arr[first + 2 * x + q, t, pl.ds(row + h, 4, stride=2), :]
                         total = part if total is None else total + part
             cstage[n, 4 * x : 4 * x + 4, :] = total * scale
 
     def coarse_send(n):
-        cedge[n, 0] = cstage[n, 0:4, :]
-        cedge[n, 1] = cstage[n, 12:16, :]
-        for x in range(4):
-            for k in range(2):
-                cedge[n, 2 + k, x : x + 1, :] = cstage[n, 4 * x + 3 * k : 4 * x + 3 * k + 1, :]
         copies = []
         for k, (dx, dy) in enumerate(NEAR):
             copies.append(
                 remote(cstage.at[n], crecv.at[n, k], cs.at[n, k], cr.at[n, k], dx, dy)
             )
             copies[-1].start()
+        cedge[n, 0] = cstage[n, 0:4, :]
+        cedge[n, 1] = cstage[n, 12:16, :]
+        for x in range(4):
+            for k in range(2):
+                cedge[n, 2 + k, x : x + 1, :] = cstage[n, 4 * x + 3 * k : 4 * x + 3 * k + 1, :]
         for k, (dx, dy) in enumerate(FAR):
             side = (dx == 2) if abs(dx) == 2 else 2 + (dy == 2)
             copies.append(
@@ -362,6 +362,7 @@
     wait(loads[0])
     pack_rows(mf, 0)
     mid_put(0, restrict_fine(mf, 1, 8, 0.125))
+    coarse_block(mid_b.at[0], 0, 0, 0, 0.125)
     wait(loads[1])
     pack_rows(px, 1)
     wait(loads[2])
@@ -394,6 +395,7 @@
     pack_rows(mf, 5, 1)
     wait_sent(m_copies)
     wait_sent(p_copies)
+    m3_copies = coarse_send(0)
     m2_copies = mid_send(0)
 
     wait_arrived(m_copies)
@@ -434,28 +436,6 @@
     mid_own(0, m2)
     wait(m2_copies)
     mid_place(0, m2)
-    coarse_block(m2, 0, 12, 0.125)
-    m3_copies = coarse_send(0)
-    wait_sent(u_copies)
-    d_copies = fine_send(d, 4, 0, 0, 0)
-
-    wait_arrived(u_copies)
-    for f in range(2):
-        k = 1 + 15 * f
-        u2[k, :, IN, :] = u2[k, :, IN, :] + gxf[f] * xr[2, f]
-        dl[f] = gyf[f] * yr[2, f]
-    add_rows(u2, 1, 8)
-    pack_rows(u2, 3)
-    u2_copies = fine_send(u2, 3)
-
-    def third_sum(i):
-        c, total = fine_sum(u2, i)
-        before = u[i + 1, :, IN, :]
-        g[i] = dg[i] * (BETA * c - GAMMA * before) + total
-        px[i + 1, :, IN, :] = px[i + 1, :, IN, :] + before + c
-
-    planes(0, 16, 4, third_sum)
-
     def mid_coefficients(i):
         c = m2[i, :, IN, :]
         below = 0.5 * (c + m2[i - 1, :, IN, :])
@@ -479,22 +459,31 @@
     cw[1:13] = 0.8 / (S3 + 0.5 * (5.0 * mob[1:-1] + lap))
     for x in range(4):
         cstage[1, 4 * x : 4 * x + 4, :] = cw[5 + x, 5:9, :]
-    w3_copies = coarse_send(1)
     for x in range(8):
         mid_b[2, x] = w2[4 + x, :, 12:20, :]
     mid_fold(2, [mid_b[2, x] for x in range(8)])
+    wait_sent(u_copies)
+    w3_copies = coarse_send(1)
+    w2_copies = mid_send(2)
+
+    wait_arrived(u_copies)
+    for f in range(2):
+        k = 1 + 15 * f
+        u2[k, :, IN, :] = u2[k, :, IN, :] + gxf[f] * xr[2, f]
+        dl[f] = gyf[f] * yr[2, f]
+    add_rows(u2, 1, 8)
+    pack_rows(u2, 3)
+    u2_copies = fine_send(u2, 3)
+
+    def third_sum(i):
+        c, total = fine_sum(u2, i)
+        before = u[i + 1, :, IN, :]
+        g[i] = dg[i] * (BETA * c - GAMMA * before) + total
+        px[i + 1, :, IN, :] = px[i + 1, :, IN, :] + before + c
+
+    planes(0, 16, 4, third_sum)
     wait_sent(u2_copies)
-    w2_copies = mid_send(2)
-
-    wait_arrived(u2_copies)
-    for f in range(2):
-        g[15 * f] = g[15 * f] + kx[16 * f] * xr[3, f]
-        dl[f] = kyf[f] * yr[3, f]
-    add_rows(g, 0, 0)
-    mid_put(1, restrict_fine(g, 0, 0, 0.5))
-    b2_copies = mid_send(1)
-
-    pack_rows(px, 6, 1)
+    d_copies = fine_send(d, 4, 0, 0, 0)
     coarse_wait(w3_copies, 1, cw)
     weight = cw[...]
     y = jnp.ones_like(weight)
@@ -531,6 +520,18 @@
         x2[i] = va[i, :, IN, :] - (1.0 + ALPHA) * c - STEP * (w2[i, :, IN, :] * total)
 
     planes(4, 12, 4, adjoint_two)
+    wait(w2_copies)
+    mid_place(2, w2)
+
+    wait_arrived(u2_copies)
+    for f in range(2):
+        g[15 * f] = g[15 * f] + kx[16 * f] * xr[3, f]
+        dl[f] = kyf[f] * yr[3, f]
+    add_rows(g, 0, 0)
+    mid_put(1, restrict_fine(g, 0, 0, 0.5))
+    b2_copies = mid_send(1)
+
+    pack_rows(px, 6, 1)
     part = jnp.zeros((2, 8, 128), F32)
     for x in range(8):
         part = part + x2[4 + x, :, 4:12, :] * mid_b[1, x]
@@ -545,8 +546,6 @@
         sums.append(remote(ar1.at[0], ar1.at[o], as1.at[o], ar1s.at[o], o, 0))
         sums[-1].start()
     far_copies = fine_send(mf, 5, 1) + corner_send(mf, 0)
-    wait(w2_copies)
-    mid_place(2, w2)
     for f in range(2):
         xr[1, f] = xr[1, f] + xr[2, f] + xr[3, f]
         yr[1, f] = yr[1, f] + yr[2, f] + yr[3, f]
@@ -572,7 +571,7 @@
         rr[i] = d2[i] * (BETA * c - GAMMA * va[i, :, IN, :]) + total
 
     planes(4, 12, 4, mid_three)
-    coarse_block(rr, 2, 4, 0.5)
+    coarse_block(rr, 2, 4, 4, 0.5)
     b3_copies = coarse_send(2)
 
     wait(sums)

time: 49.5 us -> 50.1 us (1.012)
  Pallas kernels: 48.5 us -> 49.1 us
    pallas_call x1, Pallas kernels: 48.5 us -> 49.1 us  [local(): pl.pallas_call(functools.partial(kernel, nx, ny), out_shape=jax.ShapeDtyp...]
where the time goes in v4:
time: 50.1 us; the launch traced here: 49.9 us
  Pallas kernels  49.1 us (98%)
  local copies, waits for them, and re-layouts  0.8 us (2%)
    pallas_call x1, Pallas kernels, local(): pl.pallas_call(functools.partial(kernel, nx, ny), out_shape=jax.ShapeDtyp...  49.1 us

profile of v4, /device:TPU:1, one launch (start us, length us, event | category | flops | bytes accessed | tf_op | source)
XLA Modules:
  0.0 49.9 jit_solution(7366444235659100320)
XLA Ops:
  0.0 49.1 %shard_map.37 = f32[16,16,512]{2,1,0:T(8,128)S(1)} custom-call(f32[16,16,512]{2,1,0:T(8,128)} %p_hbm.1, f32[16,16,512]{2,1,0:T(8,128)} %d_hbm.1, f32[16,16,512]{2,1,0:T(8,128)} %m_hbm.1), custom_call_target="tpu_custom_call" | custom-call | tf_op jit(solution)/shard_map/pallas_call | solution.py:751
  49.1 0.8 %copy.5 = f32[16,16,512]{2,1,0:T(8,128)} copy(f32[16,16,512]{2,1,0:T(8,128)S(1)} %shard_map.37) | data formatting | bytes 1048576

commit v5 on v2

--- a/solution.py
+++ b/solution.py
@@ -94,6 +94,7 @@
     base, fstage, frecv, fk,
     ar1, ar2,
     cst, crn, vf, v2f, ktf, k12f, kzf, wf, uf, bcs, bcr,
+    nst, nrx, nry, nrc, ring, ringr, pcor,
     in_sem, fs, fr, ms, mr, cs, cr, xs, xrs, as1, ar1s, as2, ar2s,
 ):
     gx = lax.axis_index("gx")
@@ -220,17 +221,61 @@
         return exact_dot(rs[...], tmat[...])
 
     def mid_put(n, got):
-        low = lax.broadcasted_iota(jnp.int32, (2, 8, 128), 1) < 4
         blocks = []
         for x in range(8):
             rows = got[8 * x : 8 * x + 8]
             v = jnp.stack([rows[:, :128], rows[:, 128:]], axis=0)
             mid_b[n, x] = v
             blocks.append(v)
+        return blocks
+
+    def mid_fold(n, blocks):
+        low = lax.broadcasted_iota(jnp.int32, (2, 8, 128), 1) < 4
         for t in range(4):
             a, b = blocks[2 * t], blocks[2 * t + 1]
             mid_stage[n, 0, t] = jnp.where(low, a, pltpu.roll(b, 4, 1))
             mid_stage[n, 1, t] = jnp.where(low, pltpu.roll(a, 4, 1), b)
+
+    def rhs_send():
+        for q in range(2):
+            for k in range(4):
+                for j in range(2):
+                    nst[j, q, :, 2 * k : 2 * k + 2, :] = mid_b[
+                        1, 4 * q + k, :, 6 * j : 6 * j + 2, :
+                    ]
+        copies = [
+            remote(mid_b.at[1, 0:2], nrx.at[1], ms.at[1, 0], mr.at[1, 0], -1, 0),
+            remote(mid_b.at[1, 6:8], nrx.at[0], ms.at[1, 1], mr.at[1, 1], 1, 0),
+            remote(nst.at[0], nry.at[1], ms.at[1, 2], mr.at[1, 2], 0, -1),
+            remote(nst.at[1], nry.at[0], ms.at[1, 3], mr.at[1, 3], 0, 1),
+        ]
+        k = 4
+        for i, dx in enumerate((-1, 1)):
+            for j, dy in enumerate((-1, 1)):
+                copies.append(
+                    remote(
+                        nst.at[j, i], nrc.at[1 - i, 1 - j], ms.at[1, k], mr.at[1, k], dx, dy
+                    )
+                )
+                k += 1
+        for c in copies:
+            c.start()
+        return copies
+
+    def rhs_place():
+        for i in range(2):
+            for x in range(2):
+                plane = 2 + 10 * i + x
+                b2[plane, :, 12:20, :] = nrx[i, x]
+                at = 4 - 4 * i + 2 * x
+                for j in range(2):
+                    row = 10 + 10 * j
+                    b2[plane, :, row : row + 2, :] = nrc[i, j, :, at : at + 2, :]
+        for j in range(2):
+            row = 10 + 10 * j
+            for q in range(2):
+                for k in range(4):
+                    b2[4 + 4 * q + k, :, row : row + 2, :] = nry[j, q, :, 2 * k : 2 * k + 2, :]
 
     def mid_send(n):
         copies = [
@@ -328,7 +373,7 @@
 
     wait(loads[0])
     pack_rows(mf, 0)
-    mid_put(0, restrict_fine(mf, 1, 8, 0.125))
+    mid_fold(0, mid_put(0, restrict_fine(mf, 1, 8, 0.125)))
     wait(loads[1])
     pack_rows(px, 1)
     wait(loads[2])
@@ -404,7 +449,6 @@
     coarse_block(m2, 0, 12, 0.125)
     m3_copies = coarse_send(0)
     wait_sent(u_copies)
-    d_copies = fine_send(d, 4, 0, 0, 0)
 
     wait_arrived(u_copies)
     for f in range(2):
@@ -448,7 +492,6 @@
         cstage[1, 4 * x : 4 * x + 4, :] = cw[4 + x, 4:8, :]
     w3_copies = coarse_send(1)
     wait_sent(u2_copies)
-    far_copies = fine_send(mf, 5, 1) + corner_send(mf, 0)
 
     wait_arrived(u2_copies)
     for f in range(2):
@@ -456,7 +499,7 @@
         dl[f] = kyf[f] * yr[3, f]
     add_rows(g, 0, 0)
     mid_put(1, restrict_fine(g, 0, 0, 0.5))
-    b2_copies = mid_send(1)
+    b2_copies = rhs_send()
 
     pack_rows(px, 6, 1)
     def response_one(i):
@@ -488,14 +531,15 @@
         yr[1, f] = yr[1, f] + yr[2, f] + yr[3, f]
     mid_own(1, b2)
     wait_sent(b2_copies)
-    x1_copies = fine_send(px, 6, 1) + corner_send(px, 1)
+    d_copies = fine_send(d, 4, 0, 0, 0)
+    far_copies = fine_send(mf, 5, 1) + corner_send(mf, 0)
     wait_arrived(b2_copies)
-    mid_place(1, b2)
+    rhs_place()
 
     def mid_one(i):
         va[i, :, IN, :] = w2[i] * b2[i, :, IN, :]
 
-    planes(1, 15, 7, mid_one)
+    planes(2, 14, 6, mid_one)
 
     def mid_two(i):
         c, total = mid_sum(va, i)
@@ -503,7 +547,7 @@
         vb[i, :, IN, :] = step
         x2[i] = c + step
 
-    planes(2, 14, 6, mid_two)
+    planes(3, 13, 5, mid_two)
 
     def mid_three(i):
         c, total = mid_sum(vb, i)
@@ -512,6 +556,17 @@
     planes(4, 12, 4, mid_three)
     coarse_block(rr, 2, 4, 0.5)
     b3_copies = coarse_send(2)
+    for f in range(2):
+        k = 5 + 5 * f
+        ring[f] = x2[k, :, 4:12, :]
+        for x in range(8):
+            ring[2 + f, :, x : x + 1, :] = x2[4 + x, :, k : k + 1, :]
+    ring_copies = [
+        remote(ring.at[f], ringr.at[f + 1 - 2 * (f % 2)], xs.at[8 + f], xrs.at[8 + f], ox, oy)
+        for f, (ox, oy) in enumerate(NEAR[:4])
+    ]
+    for c in ring_copies:
+        c.start()
 
     part = jnp.zeros((1, 128), F32)
     partm = jnp.zeros((1, 128), F32)
@@ -527,30 +582,7 @@
         sums.append(remote(ar1.at[0], ar1.at[o], as1.at[o], ar1s.at[o], o, 0))
         sums[-1].start()
 
-    wait(d_copies)
-    wait(far_copies)
-
-    def corners(f):
-        return ((0, 1), (2, 3), (0, 2), (1, 3))[f]
-
-    for f in range(4):
-        first, second = (xr.at[0, f], xr.at[5, f]) if f < 2 else (yr.at[0, f - 2], yr.at[5, f - 2])
-        k01 = kx[16 * f] if f < 2 else kyf[f - 2]
-        c = first[...]
-        vf[f, :, IN, :] = c
-        for row, k in zip((7, 24), corners(f)):
-            for t in range(4):
-                vf[f, t, row : row + 1, :] = crn[0, k, t : t + 1, :]
-        ktf[f, :, IN, :] = 0.5 * (c + vf[f, :, HI, :])
-        ktf[f, :, 7:8, :] = 0.5 * (vf[f, :, 7:8, :] + vf[f, :, 8:9, :])
-        k12 = 0.5 * (c + second[...])
-        after = 0.5 * (c + fine_next(c))
-        k12f[f] = k12
-        kzf[f] = after
-        wf[f] = INV / (
-            S1 + k01 + k12 + ktf[f, :, IN, :] + ktf[f, :, LO, :] + after + fine_before(after)
-        )
-
+    x1_copies = fine_send(px, 6, 1) + corner_send(px, 1)
     coarse_wait(b3_copies, 2, cb)
     rhs = cb[...]
     e = weight * rhs
@@ -569,6 +601,12 @@
         sums.append(remote(ar2.at[0], ar2.at[o], as2.at[o], ar2s.at[o], 0, o))
         sums[-1].start()
 
+    wait(ring_copies)
+    for f in range(2):
+        x2[2 + 11 * f, :, 4:12, :] = ringr[f]
+        row = 2 + 11 * f
+        for x in range(8):
+            x2[4 + x, :, row : row + 1, :] = ringr[2 + f, :, x : x + 1, :]
     ce[3:9] = e
     for x in range(6):
         for h in range(2):
@@ -609,7 +647,31 @@
         )
     for c in x_copies:
         c.start()
-    wait(x1_copies)
+
+    wait(d_copies)
+    wait(far_copies)
+
+    def corners(f):
+        return ((0, 1), (2, 3), (0, 2), (1, 3))[f]
+
+    for f in range(4):
+        first, second = (xr.at[0, f], xr.at[5, f]) if f < 2 else (yr.at[0, f - 2], yr.at[5, f - 2])
+        k01 = kx[16 * f] if f < 2 else kyf[f - 2]
+        c = first[...]
+        vf[f, :, IN, :] = c
+        for row, k in zip((7, 24), corners(f)):
+            for t in range(4):
+                vf[f, t, row : row + 1, :] = crn[0, k, t : t + 1, :]
+        ktf[f, :, IN, :] = 0.5 * (c + vf[f, :, HI, :])
+        ktf[f, :, 7:8, :] = 0.5 * (vf[f, :, 7:8, :] + vf[f, :, 8:9, :])
+        k12 = 0.5 * (c + second[...])
+        after = 0.5 * (c + fine_next(c))
+        k12f[f] = k12
+        kzf[f] = after
+        wf[f] = INV / (
+            S1 + k01 + k12 + ktf[f, :, IN, :] + ktf[f, :, LO, :] + after + fine_before(after)
+        )
+
     wait(sums)
     total = ar2[0]
     for o in range(1, ny):
@@ -623,19 +685,14 @@
         v = base[x] + kappa * xk[4 + x, :, 4:12, :]
         pout[8 * x : 8 * x + 8, 0:128] = v[0]
         pout[8 * x : 8 * x + 8, 128:256] = v[1]
-    wait(x_copies)
+    wait(x_copies[:4])
     for f in range(4):
         v = frecv[f] + kappa * fk[f]
         pout[64 + 8 * f : 72 + 8 * f, 0:128] = v[0]
         pout[64 + 8 * f : 72 + 8 * f, 128:256] = v[1]
-    for k in range(4):
-        x, y = 3 + 9 * (k // 2), 3 + 9 * (k % 2)
-        for t in range(2):
-            pout[96 + k : 97 + k, 128 * t : 128 * t + 128] = (
-                bcr[k, t : t + 1, :] + kappa * xk[x, t, y : y + 1, :]
-            )
     pout[...] = exact_dot(pout[:, 0:256], pmat[...])
 
+    wait_sent(x1_copies)
     for j in range(8):
         for t in range(4):
             v = pout[8 * j : 8 * j + 8, 128 * t : 128 * t + 128]
@@ -644,22 +701,50 @@
                     rows = pl.ds(8 + h, 8, stride=2)
                     px[2 * j + 1 + q, t, rows, :] = px[2 * j + 1 + q, t, rows, :] + v
     for f in range(4):
-        first, second = (xr.at[1, f], xr.at[6, f]) if f < 2 else (yr.at[1, f - 2], yr.at[6, f - 2])
+        first = xr.at[1, f] if f < 2 else yr.at[1, f - 2]
         for t in range(4):
             lanes = slice(128 * t, 128 * t + 128)
             v = pout[64 + 8 * f : 72 + 8 * f, lanes]
             for h in range(2):
                 rows = pl.ds(h, 8, stride=2)
                 vf[f, t, pl.ds(8 + h, 8, stride=2), :] = first[t, rows, :] + v
-                v2f[f, t, rows, :] = second[t, rows, :] + v
-            for row, k in zip((7, 24), corners(f)):
-                vf[f, t, row : row + 1, :] = crn[1, k, t : t + 1, :] + pout[96 + k : 97 + k, lanes]
     pack_rows(px, 1)
     for f in range(2):
         d[15 * f] = d[15 * f] + kx[16 * f] * vf[f, :, IN, :]
         dl[f] = kyf[f] * vf[2 + f, :, IN, :]
     add_rows(d, 0, 0)
 
+    def fourth_sum(i):
+        c, total = fine_sum(px, i)
+        u[i + 1, :, IN, :] = w[i] * (d[i] + total) - INV * c
+
+    planes(0, 16, 4, fourth_sum)
+
+    def last_sum(i):
+        c, total = fine_sum(u, i)
+        g[i] = px[i + 1, :, IN, :] + (1.0 + ALPHA) * c + STEP * (w[i] * total)
+
+    planes(0, 16, 4, last_sum)
+
+    wait_arrived(x1_copies)
+    wait(x_copies[4:])
+    for k in range(4):
+        x, y = 3 + 9 * (k // 2), 3 + 9 * (k % 2)
+        for t in range(2):
+            pcor[k : k + 1, 128 * t : 128 * t + 128] = (
+                bcr[k, t : t + 1, :] + kappa * xk[x, t, y : y + 1, :]
+            )
+    pcor[...] = exact_dot(pcor[:, 0:256], pmat[...])
+    for f in range(4):
+        second = xr.at[6, f] if f < 2 else yr.at[6, f - 2]
+        for t in range(4):
+            lanes = slice(128 * t, 128 * t + 128)
+            v = pout[64 + 8 * f : 72 + 8 * f, lanes]
+            for h in range(2):
+                rows = pl.ds(h, 8, stride=2)
+                v2f[f, t, rows, :] = second[t, rows, :] + v
+            for row, k in zip((7, 24), corners(f)):
+                vf[f, t, row : row + 1, :] = crn[1, k, t : t + 1, :] + pcor[k : k + 1, lanes]
     for f in range(4):
         if f < 2:
             k01, inside, rhs_f = kx[16 * f], px[1 + 15 * f, :, IN, :], xr[4, f]
@@ -672,17 +757,6 @@
         total = total + z * fine_next(c) + fine_before(z * c)
         uf[f] = wf[f] * (rhs_f + total) - INV * c
 
-    def fourth_sum(i):
-        c, total = fine_sum(px, i)
-        u[i + 1, :, IN, :] = w[i] * (d[i] + total) - INV * c
-
-    planes(0, 16, 4, fourth_sum)
-
-    def last_sum(i):
-        c, total = fine_sum(u, i)
-        g[i] = px[i + 1, :, IN, :] + (1.0 + ALPHA) * c + STEP * (w[i] * total)
-
-    planes(0, 16, 4, last_sum)
     for f in range(2):
         g[15 * f] = g[15 * f] + gxf[f] * uf[f]
         dl[f] = gyf[f] * uf[2 + f]
@@ -706,7 +780,7 @@
             vm(17, 4, 16, 128), vm(16, 4, 32, 128), vm(*plane),
             vm(7, 2, *face), vm(7, 2, *face), vm(7, 2, *face),
             vm(2, *face), vm(2, *face), vm(2, *face), vm(2, *face), vm(64, 512),
-            pltpu.VMEM((512, 256), BF16), pltpu.VMEM((256, 512), BF16), vm(104, 512),
+            pltpu.VMEM((512, 256), BF16), pltpu.VMEM((256, 512), BF16), vm(96, 512),
             vm(2, 8, 2, 8, 128), vm(2, 2, 4, 2, 8, 128), vm(2, 2, 4, 2, 8, 128),
             vm(2, 2, 4, 2, 8, 128), vm(2, 2, 2, 2, 2, 8, 128),
             vm(16, 2, 32, 128), vm(16, 2, 32, 128), vm(16, 2, 16, 128), vm(16, 2, 16, 128),
@@ -719,8 +793,10 @@
             vm(nx, 2, 128), vm(ny, 2, 128),
             vm(2, 4, 4, 128), vm(2, 4, 4, 128), vm(4, 4, 32, 128), vm(4, *face), vm(4, 4, 32, 128),
             vm(4, *face), vm(4, *face), vm(4, *face), vm(4, *face), vm(4, 2, 128), vm(4, 2, 128),
+            vm(2, 2, 2, 8, 128), vm(2, 2, 2, 8, 128), vm(2, 2, 2, 8, 128), vm(2, 2, 2, 8, 128),
+            vm(4, 2, 8, 128), vm(4, 2, 8, 128), vm(8, 512),
             sem(3, 4), sem(9, 4), sem(9, 4), sem(2, 8), sem(2, 8), sem(3, 8), sem(3, 8),
-            sem(8), sem(8), sem(nx), sem(nx), sem(ny), sem(ny),
+            sem(12), sem(12), sem(nx), sem(nx), sem(ny), sem(ny),
         ]
         return pl.pallas_call(
             functools.partial(kernel, nx, ny),

time: 48.3 us -> 48.2 us (level)
  no operation moved by 1% of the time
where the time goes in v5:
time: 48.2 us; the launch traced here: 48.1 us
  Pallas kernels  47.3 us (98%)
  local copies, waits for them, and re-layouts  0.8 us (2%)
    pallas_call x1, Pallas kernels, local(): pl.pallas_call(functools.partial(kernel, nx, ny), out_shape=jax.ShapeDtyp...  47.3 us

profile of v5, /device:TPU:1, one launch (start us, length us, event | category | flops | bytes accessed | tf_op | source)
XLA Modules:
  0.0 48.1 jit_solution(13806419142542346562)
XLA Ops:
  0.0 47.3 %shard_map.37 = f32[16,16,512]{2,1,0:T(8,128)S(1)} custom-call(f32[16,16,512]{2,1,0:T(8,128)} %p_hbm.1, f32[16,16,512]{2,1,0:T(8,128)} %d_hbm.1, f32[16,16,512]{2,1,0:T(8,128)} %m_hbm.1), custom_call_target="tpu_custom_call" | custom-call | tf_op jit(solution)/shard_map/pallas_call | solution.py:801
  47.3 0.8 %copy.5 = f32[16,16,512]{2,1,0:T(8,128)} copy(f32[16,16,512]{2,1,0:T(8,128)S(1)} %shard_map.37) | data formatting | bytes 1048576

commit v6 on v5

--- a/solution.py
+++ b/solution.py
@@ -428,7 +428,7 @@
         w[i] = weight
         u[i + 1, :, IN, :] = weight * g[i] - INV * px[i + 1, :, IN, :]
 
-    planes(0, 16, 4, first_step)
+    planes(0, 16, 8, first_step)
     pack_rows(u, 2)
     u_copies = fine_send(u, 2)
 
@@ -437,6 +437,7 @@
         u2[i + 1, :, IN, :] = ALPHA * c + STEP * (w[i] * total)
 
     planes(0, 16, 4, second_sum)
+    wait_sent(u_copies)
     for x in range(16):
         for f in range(2):
             gyf[f, :, x : x + 1, :] = w[x, :, 15 * f : 15 * f + 1, :]
@@ -448,7 +449,6 @@
     mid_place(0, m2)
     coarse_block(m2, 0, 12, 0.125)
     m3_copies = coarse_send(0)
-    wait_sent(u_copies)
 
     wait_arrived(u_copies)
     for f in range(2):
@@ -466,6 +466,7 @@
         px[i + 1, :, IN, :] = px[i + 1, :, IN, :] + before + c
 
     planes(0, 16, 4, third_sum)
+    wait_sent(u2_copies)
 
     def mid_coefficients(i):
         c = m2[i, :, IN, :]
@@ -491,7 +492,6 @@
     for x in range(4):
         cstage[1, 4 * x : 4 * x + 4, :] = cw[4 + x, 4:8, :]
     w3_copies = coarse_send(1)
-    wait_sent(u2_copies)
 
     wait_arrived(u2_copies)
     for f in range(2):
@@ -531,8 +531,7 @@
         yr[1, f] = yr[1, f] + yr[2, f] + yr[3, f]
     mid_own(1, b2)
     wait_sent(b2_copies)
-    d_copies = fine_send(d, 4, 0, 0, 0)
-    far_copies = fine_send(mf, 5, 1) + corner_send(mf, 0)
+    x1_copies = fine_send(px, 6, 1) + corner_send(px, 1)
     wait_arrived(b2_copies)
     rhs_place()
 
@@ -582,7 +581,8 @@
         sums.append(remote(ar1.at[0], ar1.at[o], as1.at[o], ar1s.at[o], o, 0))
         sums[-1].start()
 
-    x1_copies = fine_send(px, 6, 1) + corner_send(px, 1)
+    d_copies = fine_send(d, 4, 0, 0, 0)
+    far_copies = fine_send(mf, 5, 1) + corner_send(mf, 0)
     coarse_wait(b3_copies, 2, cb)
     rhs = cb[...]
     e = weight * rhs
@@ -718,13 +718,13 @@
         c, total = fine_sum(px, i)
         u[i + 1, :, IN, :] = w[i] * (d[i] + total) - INV * c
 
-    planes(0, 16, 4, fourth_sum)
+    planes(0, 16, 8, fourth_sum)
 
     def last_sum(i):
         c, total = fine_sum(u, i)
         g[i] = px[i + 1, :, IN, :] + (1.0 + ALPHA) * c + STEP * (w[i] * total)
 
-    planes(0, 16, 4, last_sum)
+    planes(0, 16, 8, last_sum)
 
     wait_arrived(x1_copies)
     wait(x_copies[4:])

time: 48.2 us -> 45.8 us (0.950)
  Pallas kernels: 47.3 us -> 44.4 us
    pallas_call x1, Pallas kernels: 47.3 us -> 44.4 us  [local(): pl.pallas_call(functools.partial(kernel, nx, ny), out_shape=jax.ShapeDtyp...]
where the time goes in v6:
time: 45.8 us; the launch traced here: 45.2 us
  Pallas kernels  44.4 us (97%)
  local copies, waits for them, and re-layouts  0.8 us (2%)
    pallas_call x1, Pallas kernels, local(): pl.pallas_call(functools.partial(kernel, nx, ny), out_shape=jax.ShapeDtyp...  44.4 us

profile of v6, /device:TPU:1, one launch (start us, length us, event | category | flops | bytes accessed | tf_op | source)
XLA Modules:
  0.0 45.2 jit_solution(8245624033678497073)
XLA Ops:
  0.0 44.4 %shard_map.37 = f32[16,16,512]{2,1,0:T(8,128)S(1)} custom-call(f32[16,16,512]{2,1,0:T(8,128)} %p_hbm.1, f32[16,16,512]{2,1,0:T(8,128)} %d_hbm.1, f32[16,16,512]{2,1,0:T(8,128)} %m_hbm.1), custom_call_target="tpu_custom_call" | custom-call | tf_op jit(solution)/shard_map/pallas_call | solution.py:801
  44.4 0.8 %copy.5 = f32[16,16,512]{2,1,0:T(8,128)} copy(f32[16,16,512]{2,1,0:T(8,128)S(1)} %shard_map.37) | data formatting | bytes 1048576

commit v7 on v6

--- a/solution.py
+++ b/solution.py
@@ -722,7 +722,9 @@
 
     def last_sum(i):
         c, total = fine_sum(u, i)
-        g[i] = px[i + 1, :, IN, :] + (1.0 + ALPHA) * c + STEP * (w[i] * total)
+        done = px[i + 1, :, IN, :] + (1.0 + ALPHA) * c + STEP * (w[i] * total)
+        for t in range(4):
+            out[i, :, 128 * t : 128 * t + 128] = done[t]
 
     planes(0, 16, 8, last_sum)
 
@@ -758,12 +760,17 @@
         uf[f] = wf[f] * (rhs_f + total) - INV * c
 
     for f in range(2):
-        g[15 * f] = g[15 * f] + gxf[f] * uf[f]
+        face = gxf[f] * uf[f]
         dl[f] = gyf[f] * uf[2 + f]
-    add_rows(g, 0, 0)
-    for i in range(16):
         for t in range(4):
-            out[i, :, 128 * t : 128 * t + 128] = g[i, t]
+            lanes = slice(128 * t, 128 * t + 128)
+            out[15 * f, :, lanes] = out[15 * f, :, lanes] + face[t]
+    for x in range(16):
+        for f in range(2):
+            for t in range(4):
+                lanes = slice(128 * t, 128 * t + 128)
+                k = 15 * f
+                out[x, k : k + 1, lanes] = out[x, k : k + 1, lanes] + dl[f, t, x : x + 1, :]
 
 
 def solution(mesh):

time: 45.8 us -> 45.7 us (level)
  no operation moved by 1% of the time
where the time goes in v7:
time: 45.7 us; the launch traced here: 45.2 us
  Pallas kernels  44.3 us (97%)
  local copies, waits for them, and re-layouts  0.8 us (2%)
    pallas_call x1, Pallas kernels, local(): pl.pallas_call(functools.partial(kernel, nx, ny), out_shape=jax.ShapeDtyp...  44.3 us

profile of v7, /device:TPU:1, one launch (start us, length us, event | category | flops | bytes accessed | tf_op | source)
XLA Modules:
  0.0 45.2 jit_solution(7835008267376966851)
XLA Ops:
  0.0 44.3 %shard_map.37 = f32[16,16,512]{2,1,0:T(8,128)S(1)} custom-call(f32[16,16,512]{2,1,0:T(8,128)} %p_hbm.1, f32[16,16,512]{2,1,0:T(8,128)} %d_hbm.1, f32[16,16,512]{2,1,0:T(8,128)} %m_hbm.1), custom_call_target="tpu_custom_call" | custom-call | tf_op jit(solution)/shard_map/pallas_call | solution.py:808
  44.4 0.8 %copy.5 = f32[16,16,512]{2,1,0:T(8,128)} copy(f32[16,16,512]{2,1,0:T(8,128)S(1)} %shard_map.37) | data formatting | bytes 1048576

commit v8 on v7

--- a/solution.py
+++ b/solution.py
@@ -279,8 +279,8 @@
 
     def mid_send(n):
         copies = [
-            remote(mid_b.at[n, 0:4], mid_rx.at[n, 1], ms.at[n, 0], mr.at[n, 0], -1, 0),
-            remote(mid_b.at[n, 4:8], mid_rx.at[n, 0], ms.at[n, 1], mr.at[n, 1], 1, 0),
+            remote(mid_b.at[n, 0:3], mid_rx.at[n, 1, 0:3], ms.at[n, 0], mr.at[n, 0], -1, 0),
+            remote(mid_b.at[n, 5:8], mid_rx.at[n, 0, 1:4], ms.at[n, 1], mr.at[n, 1], 1, 0),
             remote(mid_stage.at[n, 0], mid_ry.at[n, 1], ms.at[n, 2], mr.at[n, 2], 0, -1),
             remote(mid_stage.at[n, 1], mid_ry.at[n, 0], ms.at[n, 3], mr.at[n, 3], 0, 1),
         ]
@@ -300,7 +300,7 @@
 
     def mid_place(n, ext):
         for i in range(2):
-            for x in range(4):
+            for x in range(1 - i, 4 - i):
                 ext[12 * i + x, :, 12:20, :] = mid_rx[n, i, x]
             for t in range(4):
                 for q in range(2):
@@ -484,7 +484,7 @@
         d2[i] = diagonal
         w2[i] = INV / diagonal
 
-    planes(1, 15, 7, mid_coefficients)
+    planes(2, 14, 6, mid_coefficients)
     coarse_wait(m3_copies, 0, cm)
     mob = cm[...]
     lap = weighted_sum(mob)
@@ -505,13 +505,13 @@
     def response_one(i):
         vb[i, :, IN, :] = (-S2) * w2[i]
 
-    planes(1, 15, 7, response_one)
+    planes(2, 14, 6, response_one)
 
     def response_two(i):
         c, total = mid_sum(vb, i)
         xk[i] = 1.0 + (1.0 + ALPHA) * c + STEP * (w2[i] * total)
 
-    planes(2, 14, 6, response_two)
+    planes(3, 13, 5, response_two)
     for x in range(8):
         fk[2, :, x : x + 1, :] = xk[4 + x, :, 3:4, :]
         fk[3, :, x : x + 1, :] = xk[4 + x, :, 12:13, :]
@@ -555,18 +555,6 @@
     planes(4, 12, 4, mid_three)
     coarse_block(rr, 2, 4, 0.5)
     b3_copies = coarse_send(2)
-    for f in range(2):
-        k = 5 + 5 * f
-        ring[f] = x2[k, :, 4:12, :]
-        for x in range(8):
-            ring[2 + f, :, x : x + 1, :] = x2[4 + x, :, k : k + 1, :]
-    ring_copies = [
-        remote(ring.at[f], ringr.at[f + 1 - 2 * (f % 2)], xs.at[8 + f], xrs.at[8 + f], ox, oy)
-        for f, (ox, oy) in enumerate(NEAR[:4])
-    ]
-    for c in ring_copies:
-        c.start()
-
     part = jnp.zeros((1, 128), F32)
     partm = jnp.zeros((1, 128), F32)
     for x in range(4):
@@ -580,6 +568,18 @@
     for o in range(1, nx):
         sums.append(remote(ar1.at[0], ar1.at[o], as1.at[o], ar1s.at[o], o, 0))
         sums[-1].start()
+
+    for f in range(2):
+        k = 5 + 5 * f
+        ring[f] = x2[k, :, 4:12, :]
+        for x in range(8):
+            ring[2 + f, :, x : x + 1, :] = x2[4 + x, :, k : k + 1, :]
+    ring_copies = [
+        remote(ring.at[f], ringr.at[f + 1 - 2 * (f % 2)], xs.at[8 + f], xrs.at[8 + f], ox, oy)
+        for f, (ox, oy) in enumerate(NEAR[:4])
+    ]
+    for c in ring_copies:
+        c.start()
 
     d_copies = fine_send(d, 4, 0, 0, 0)
     far_copies = fine_send(mf, 5, 1) + corner_send(mf, 0)

time: 45.7 us -> 45.2 us (0.989); the launches traced: 45.2 us -> 45.1 us
  no operation moved by 1% of the time
where the time goes in v8:
time: 45.2 us; the launch traced here: 45.1 us
  Pallas kernels  44.3 us (98%)
  local copies, waits for them, and re-layouts  0.8 us (2%)
    pallas_call x1, Pallas kernels, local(): pl.pallas_call(functools.partial(kernel, nx, ny), out_shape=jax.ShapeDtyp...  44.3 us

profile of v8, /device:TPU:1, one launch (start us, length us, event | category | flops | bytes accessed | tf_op | source)
XLA Modules:
  0.0 45.1 jit_solution(8502811074005041457)
XLA Ops:
  0.0 44.3 %shard_map.37 = f32[16,16,512]{2,1,0:T(8,128)S(1)} custom-call(f32[16,16,512]{2,1,0:T(8,128)} %p_hbm.1, f32[16,16,512]{2,1,0:T(8,128)} %d_hbm.1, f32[16,16,512]{2,1,0:T(8,128)} %m_hbm.1), custom_call_target="tpu_custom_call" | custom-call | tf_op jit(solution)/shard_map/pallas_call | solution.py:808
  44.3 0.8 %copy.5 = f32[16,16,512]{2,1,0:T(8,128)} copy(f32[16,16,512]{2,1,0:T(8,128)S(1)} %shard_map.37) | data formatting | bytes 1048576

commit v9 on v8

--- a/solution.py
+++ b/solution.py
@@ -401,7 +401,7 @@
         c, total = fine_sum(px, i)
         g[i] = d[i] + total
 
-    planes(0, 16, 4, first_sum)
+    planes(0, 16, 8, first_sum)
     pack_rows(d, 4, 0, 0, 0)
     pack_rows(mf, 5, 1)
     wait_sent(m_copies)
@@ -436,7 +436,7 @@
         c, total = fine_sum(u, i)
         u2[i + 1, :, IN, :] = ALPHA * c + STEP * (w[i] * total)
 
-    planes(0, 16, 4, second_sum)
+    planes(0, 16, 8, second_sum)
     wait_sent(u_copies)
     for x in range(16):
         for f in range(2):
@@ -465,7 +465,7 @@
         g[i] = dg[i] * (BETA * c - GAMMA * before) + total
         px[i + 1, :, IN, :] = px[i + 1, :, IN, :] + before + c
 
-    planes(0, 16, 4, third_sum)
+    planes(0, 16, 8, third_sum)
     wait_sent(u2_copies)
 
     def mid_coefficients(i):

time: 45.2 us -> 45.2 us (level)
  no operation moved by 1% of the time
where the time goes in v9:
time: 45.2 us; the launch traced here: 45.1 us
  Pallas kernels  44.3 us (98%)
  local copies, waits for them, and re-layouts  0.8 us (2%)
    pallas_call x1, Pallas kernels, local(): pl.pallas_call(functools.partial(kernel, nx, ny), out_shape=jax.ShapeDtyp...  44.3 us

profile of v9, /device:TPU:1, one launch (start us, length us, event | category | flops | bytes accessed | tf_op | source)
XLA Modules:
  0.0 45.1 jit_solution(10326261403352569685)
XLA Ops:
  0.0 44.3 %shard_map.37 = f32[16,16,512]{2,1,0:T(8,128)S(1)} custom-call(f32[16,16,512]{2,1,0:T(8,128)} %p_hbm.1, f32[16,16,512]{2,1,0:T(8,128)} %d_hbm.1, f32[16,16,512]{2,1,0:T(8,128)} %m_hbm.1), custom_call_target="tpu_custom_call" | custom-call | tf_op jit(solution)/shard_map/pallas_call | solution.py:808
  44.3 0.8 %copy.5 = f32[16,16,512]{2,1,0:T(8,128)} copy(f32[16,16,512]{2,1,0:T(8,128)S(1)} %shard_map.37) | data formatting | bytes 1048576
